TPU v7x, 32 devices: a whole 2x2x4 slice. The times are simulated.
32 devices in a mesh: wide: 8 (over z, x), narrow: 4 (over y, core).
Axes of the slice: x: 2, y: 2, z: 4, core: 2. Of those that a mesh axis runs over, the one named last changes fastest.
Arguments:
- dens_tiles: bfloat16 [512, 3, 128, 128], P(('wide', 'narrow')), may hold values from -6 to 6
- tile_dest: int32 [512, 2], P(('wide', 'narrow')), may hold values from 0 to 7, all different within a row; in each aligned block of 16 rows (0 to 15, 16 to 31, ...) at most 8 rows name the same one
- tile_place: int32 [512, 2], P(('wide', 'narrow')), may hold values from 0 to 49
- tile_rows: int32 [512], P(('wide', 'narrow')), may hold values from 0 to 15
- tile_cols: int32 [512], P(('wide', 'narrow')), may hold values from 0 to 31
- ao_values: bfloat16 [16, 640, 1280], P('wide'), may hold values from -0.25 to 0.25
- point_count: int32 [16], P('wide'), may hold values from 1 to 1280, 12800 in all
- weights: float32 [16, 1280], P('wide'), may hold values from 0.05 to 1
- kernel_first: float32 [16, 1280], P('wide'), may hold values from -1.5 to -0.3
- kernel_second: float32 [16, 1280], P('wide'), may hold values from 0.2 to 2
- occ_coef: bfloat16 [16384, 512], P('wide'), may hold values from -0.3125 to 0.3125
- vir_coef: bfloat16 [16384, 1024], P('narrow'), may hold values from -0.3125 to 0.3125
Outputs:
- response: float32 [3, 512, 1024], P(None, 'wide', 'narrow')
Inputs may be any that keep to these rules, and one draw needn't show every extreme that they name: `tile_dest`: among the routes of one device's 16 tiles, no wide index is named more than 8 times, and some device names some index exactly 8 times; the 2 indices of one tile differ. `point_count`: the counts of all batches sum to 12800.
All inputs are finite; a program needn't handle non-finite values. No bound on the sum of `point_count` on one device may be relied on, other than what follows from the above.
Results may differ from a plain program's by a relative error of at most 0.0074.
Values may be sent and summed in bfloat16 or wider, within the bound.
No kernel may reach another device: no remote copies, remote signals or barrier semaphores. Data moves between devices by JAX's collectives and lax.ppermute only.
A program may use at most 128 MiB of HBM per device.

v0:
```python
import functools

import jax
import jax.numpy as jnp
from jax import lax
from jax.experimental import pallas as pl
from jax.experimental.pallas import tpu as pltpu
from jax.sharding import PartitionSpec as P


BLK = 128
KB = 5
FIELDS = 3
TOP = 2
NBAT = 2
ANY = pl.BlockSpec(memory_space=pl.ANY)
VMEM = pl.BlockSpec(memory_space=pltpu.VMEM)
SMEM = pl.BlockSpec(memory_space=pltpu.SMEM)


def density_kernel(count, groups, slot_ref, dest_ref, row_ref, col_ref, *refs):
    ao_refs = refs[:count]
    tile_refs = refs[count : count + groups]
    out_ref, held, sems = refs[count + groups :]
    copies = [pltpu.make_async_copy(ao_refs[i], held.at[i], sems.at[i]) for i in range(count)]
    for copy in copies:
        copy.start()
    out_ref[...] = jnp.zeros_like(out_ref)
    for copy in copies:
        copy.wait()
    tiles = tile_refs[0].shape[0]
    points = held.shape[2]
    for group in range(groups):
        tile_ref = tile_refs[group]

        def step(i, carry, group=group, tile_ref=tile_ref):
            at = group * tiles * TOP + i
            slot = slot_ref[at]

            @pl.when(slot >= 0)
            def _():
                left = tile_ref[i // TOP]
                rows = pl.ds(pl.multiple_of(row_ref[at] * BLK, BLK), BLK)
                cols = pl.ds(pl.multiple_of(col_ref[at] * BLK, BLK), BLK)
                dest = dest_ref[at]
                for low in range(0, points, 256):
                    lanes = slice(low, min(low + 256, points))
                    mixed = jnp.dot(left, held[slot, cols, lanes], preferred_element_type=jnp.float32)
                    mixed = mixed.reshape(FIELDS, BLK, mixed.shape[-1])
                    value = held[slot, rows, lanes].astype(jnp.float32)
                    out_ref[dest, :, lanes] += jnp.sum(mixed * value[None], axis=1)

            return carry

        lax.fori_loop(0, tiles * TOP, step, 0)


def density_call(slots, dests, rows, cols, ao_list, tile_list, wide_count):
    count, groups = len(ao_list), len(tile_list)
    height, points = ao_list[0].shape
    return pl.pallas_call(
        functools.partial(density_kernel, count, groups),
        out_shape=jax.ShapeDtypeStruct((wide_count, FIELDS, points), jnp.float32),
        in_specs=[SMEM] * 4 + [ANY] * count + [VMEM] * groups,
        out_specs=VMEM,
        scratch_shapes=[
            pltpu.VMEM((count, height, points), jnp.bfloat16),
            pltpu.SemaphoreType.DMA((count,)),
        ],
        compiler_params=pltpu.CompilerParams(vmem_limit_bytes=24 * 1024 * 1024),
        cost_estimate=pl.CostEstimate(
            flops=1_000_000_000, bytes_accessed=10_000_000, transcendentals=0
        ),
        name="density",
    )(slots, dests, rows, cols, *ao_list, *tile_list)


def block_kernel(count, groups, first, place_ref, slot_ref, row_ref, col_ref, pot_ref, *refs):
    ao_refs = refs[:count]
    out_refs = refs[count : count + groups * FIELDS]
    held, total, sems = refs[count + groups * FIELDS :]

    def each(act):
        for i in range(count):

            @pl.when(place_ref[i] >= 0)
            def _():
                act(pltpu.make_async_copy(ao_refs[i], held.at[place_ref[i]], sems.at[i]))

    each(lambda copy: copy.start())
    each(lambda copy: copy.wait())
    tiles = out_refs[0].shape[0]
    for group in range(groups):

        def step(t, carry, group=group):
            total[...] = jnp.zeros_like(total)
            for k in range(TOP):
                at = ((first + group) * tiles + t) * TOP + k
                slot = slot_ref[at]

                @pl.when(slot >= 0)
                def _():
                    rows = pl.ds(pl.multiple_of(row_ref[at] * BLK, BLK), BLK)
                    cols = pl.ds(pl.multiple_of(col_ref[at] * BLK, BLK), BLK)
                    value = held[slot, rows, :].astype(jnp.float32)
                    right = held[slot, cols, :]
                    for f in range(FIELDS):
                        scaled = (value * pot_ref[slot, f : f + 1, :]).astype(jnp.bfloat16)
                        total[f] += lax.dot_general(
                            scaled,
                            right,
                            (((1,), (1,)), ((), ())),
                            preferred_element_type=jnp.float32,
                        )

            for f in range(FIELDS):
                out_refs[group * FIELDS + f][t] = total[f].astype(jnp.bfloat16)
            return carry

        lax.fori_loop(0, tiles, step, 0)


def block_call(first, groups, places, slots, rows, cols, potential, ao_list, tiles):
    count = len(ao_list)
    height, points = ao_list[0].shape
    wide_count = potential.shape[0]
    outs = pl.pallas_call(
        functools.partial(block_kernel, count, groups, first),
        out_shape=[jax.ShapeDtypeStruct((tiles, BLK, BLK), jnp.bfloat16)] * (groups * FIELDS),
        in_specs=[SMEM] * 4 + [VMEM] + [ANY] * count,
        out_specs=[VMEM] * (groups * FIELDS),
        scratch_shapes=[
            pltpu.VMEM((wide_count, height, points), jnp.bfloat16),
            pltpu.VMEM((FIELDS, BLK, BLK), jnp.float32),
            pltpu.SemaphoreType.DMA((count,)),
        ],
        compiler_params=pltpu.CompilerParams(vmem_limit_bytes=40 * 1024 * 1024),
        cost_estimate=pl.CostEstimate(
            flops=2_000_000_000 * groups, bytes_accessed=10_000_000, transcendentals=0
        ),
        name="blocks",
    )(places, slots, rows, cols, potential, *ao_list)
    return [outs[g * FIELDS : (g + 1) * FIELDS] for g in range(groups)]


def project_kernel(parts, where_ref, *refs):
    part_refs = refs[:parts]
    occ_ref, vir_ref, even_ref, odd_ref, left_ref = refs[parts:]
    wide_at, narrow_at, wide_count = where_ref[0], where_ref[1], where_ref.shape[0] - 2
    tiles, nocc = occ_ref.shape[:2]
    owned = nocc // wide_count
    pieces = even_ref.shape[0] + odd_ref.shape[0]
    width = vir_ref.shape[1] // pieces

    def fill(t, carry):
        block = part_refs[0][t].astype(jnp.float32)
        for ref in part_refs[1:]:
            block += ref[t].astype(jnp.float32)
        left = jnp.dot(
            occ_ref[t], block.astype(jnp.bfloat16), preferred_element_type=jnp.float32
        ).astype(jnp.bfloat16)
        lanes = pl.ds(pl.multiple_of(t * BLK, BLK), BLK)
        for q in range(wide_count):
            at = pl.multiple_of((wide_at ^ q) * owned, owned)
            left_ref[pl.ds(at, owned), lanes] = left[q * owned : (q + 1) * owned]
        return carry

    lax.fori_loop(0, tiles, fill, 0)
    for j in range(pieces):
        lanes = pl.ds(pl.multiple_of((narrow_at ^ j) * width, width), width)
        value = jnp.dot(left_ref[...], vir_ref[:, lanes], preferred_element_type=jnp.float32)
        if j % 2:
            odd_ref[j // 2] = value.astype(jnp.bfloat16)
        else:
            even_ref[j // 2] = value


def project_call(where, part_list, occ_sel, vir_sel, narrow_count):
    _, nocc = occ_sel.shape[:2]
    depth, nvir = vir_sel.shape
    shape = (narrow_count // 2, nocc, nvir // narrow_count)
    return pl.pallas_call(
        functools.partial(project_kernel, len(part_list)),
        out_shape=[
            jax.ShapeDtypeStruct(shape, jnp.float32),
            jax.ShapeDtypeStruct(shape, jnp.bfloat16),
        ],
        in_specs=[SMEM] + [VMEM] * (len(part_list) + 2),
        out_specs=[VMEM] * 2,
        scratch_shapes=[pltpu.VMEM((nocc, depth), jnp.bfloat16)],
        compiler_params=pltpu.CompilerParams(vmem_limit_bytes=32 * 1024 * 1024),
        cost_estimate=pl.CostEstimate(
            flops=2_400_000_000, bytes_accessed=10_000_000, transcendentals=0
        ),
        name="project",
    )(where, *part_list, occ_sel, vir_sel)


def body(
    dens_tiles,
    tile_dest,
    tile_place,
    tile_rows,
    tile_cols,
    ao_values,
    point_count,
    weights,
    kernel_first,
    kernel_second,
    occ_coef,
    vir_coef,
):
    wide_count = lax.axis_size("wide")
    narrow_count = lax.axis_size("narrow")
    tile_count = dens_tiles.shape[0]
    nocc, nvir = occ_coef.shape[1], vir_coef.shape[1]
    halves = narrow_count // NBAT
    points = ao_values.shape[2] // halves
    line = wide_count // 2
    wide = lax.axis_index("wide")
    narrow = lax.axis_index("narrow")
    batch, half = narrow // halves, narrow % halves
    level = wide // 2

    def across(x, least=0, most=line - 1):
        pairs = [(i, i ^ 1) for i in range(wide_count) if least <= i // 2 <= most]
        return lax.ppermute(x, "wide", pairs)

    def upward(x, k):
        return lax.ppermute(
            x, "wide", [(i, i + 2) for i in range(wide_count - 2) if i // 2 >= k - 1]
        )

    def downward(x, k):
        return lax.ppermute(
            x, "wide", [(i, i - 2) for i in range(2, wide_count) if i // 2 <= line - k]
        )

    def beside(x, mask):
        return lax.ppermute(x, "narrow", [(i, i ^ mask) for i in range(narrow_count)])

    own = lax.dynamic_slice(
        ao_values, (batch, 0, half * points), (1, ao_values.shape[1], points)
    )[0]
    up, down = {0: own}, {0: own}
    own_beside = across(own)
    ao_stages = [[own, own_beside]]
    ao_places = [wide, wide ^ 1]
    tiles = dens_tiles.reshape(tile_count, FIELDS * BLK, BLK)
    for k in range(1, line):
        up[k] = upward(up[k - 1], k)
        down[k] = downward(down[k - 1], k)
        up_beside = across(up[k], least=k)
        down_beside = across(down[k], most=line - 1 - k)
        ao_stages.append([up[k], up_beside, down[k], down_beside])
        low_ok, high_ok = level >= k, level + k < line
        ao_places += [
            jnp.where(low_ok, wide - 2 * k, -1),
            jnp.where(low_ok, (wide - 2 * k) ^ 1, -1),
            jnp.where(high_ok, wide + 2 * k, -1),
            jnp.where(high_ok, (wide + 2 * k) ^ 1, -1),
        ]
    routes = jnp.stack([tile_dest, tile_place]).reshape(1, -1)
    routes = lax.all_to_all(
        jnp.broadcast_to(routes, (narrow_count, routes.shape[1])),
        "narrow",
        split_axis=0,
        concat_axis=0,
        tiled=True,
    )
    tiles, routes = lax.optimization_barrier((tiles, routes))
    tile_list = [tiles]
    mask = narrow_count // 2
    while mask:
        pairs = []
        for x in tile_list:
            pairs += [x, beside(x, mask)]
        tile_list = pairs
        mask //= 2

    routes = jnp.take(routes, narrow ^ jnp.arange(narrow_count), axis=0)
    routes = routes.reshape(narrow_count, 2, tile_count * TOP)
    dests, places = routes[:, 0].reshape(-1), routes[:, 1].reshape(-1)
    mine = places // (KB * KB) == batch
    rows = places % (KB * KB) // KB
    cols = places % KB
    offset = dests // 2 - level
    other = (dests ^ wide) & 1
    occ_sel = occ_coef.reshape(-1, BLK, nocc)[tile_rows].transpose(0, 2, 1)
    vir_sel = vir_coef.reshape(-1, BLK, nvir)[tile_cols].reshape(tile_count * BLK, nvir)
    dests, occ_sel, vir_sel = lax.optimization_barrier((dests, occ_sel, vir_sel))
    density = None
    for k in range(line):
        index = other + 2 * (offset > 0).astype(jnp.int32) if k else other
        slots = jnp.where(mine & (jnp.abs(offset) == k), index, -1)
        if density is not None:
            slots, density = lax.optimization_barrier((slots, density))
        part = density_call(slots, dests, rows, cols, ao_stages[k], tile_list, wide_count)
        density = part if density is None else density + part
    density = lax.all_to_all(density, "wide", split_axis=0, concat_axis=0, tiled=True)
    density = jnp.sum(density, axis=0)

    def here(x):
        return lax.dynamic_slice(x, (batch, half * points), (1, points))

    used = lax.dynamic_slice(point_count, (batch,), (1,))
    inside = (half * points + jnp.arange(points))[None, :] < used[:, None]
    scale = jnp.where(inside, here(weights), jnp.float32(0.0))
    first, second = here(kernel_first), here(kernel_second)
    product = jnp.stack([density[1] * density[2], density[0] * density[2], density[0] * density[1]])
    potential = (first * density + second * product) * scale
    potential = lax.all_to_all(
        jnp.broadcast_to(potential[None], (wide_count,) + potential.shape),
        "wide",
        split_axis=0,
        concat_axis=0,
        tiled=True,
    )
    ao_list = [x for stage in ao_stages for x in stage]
    held_places = jnp.stack(ao_places)
    kept = jnp.where(mine, dests, -1)
    where = jnp.concatenate([jnp.stack([wide, narrow]), jnp.zeros((wide_count,), jnp.int32)])

    half_count = narrow_count // 2
    far = block_call(
        half_count, half_count, held_places, kept, rows, cols, potential, ao_list, tile_count
    )

    def fold(groups):
        mask = 1
        while len(groups) > 1:
            groups = [
                [
                    (p.astype(jnp.float32) + beside(q, mask).astype(jnp.float32)).astype(
                        jnp.bfloat16
                    )
                    for p, q in zip(groups[i], groups[i + 1])
                ]
                for i in range(0, len(groups), 2)
            ]
            mask *= 2
        return groups[0]

    far_sum = fold(far)
    potential, far_sum = lax.optimization_barrier((potential, far_sum))
    far_parts = []
    for f in range(FIELDS):
        far_parts.append(beside(far_sum[f], half_count))
    far_sum = far_parts
    near = block_call(0, half_count, held_places, kept, rows, cols, potential, ao_list, tile_count)
    near_sum = fold(near)
    results = []
    for f in range(FIELDS):
        even, odd = project_call(where, [near_sum[f], far_sum[f]], occ_sel, vir_sel, narrow_count)
        mask = 1
        while True:
            even = even + beside(odd, mask).astype(jnp.float32)
            mask *= 2
            if mask == narrow_count:
                break
            even = even.reshape((-1, 2) + even.shape[1:])
            even, odd = even[:, 0], even[:, 1].astype(jnp.bfloat16)
        value = even.reshape(wide_count, nocc // wide_count, nvir // narrow_count)
        mask = 1
        while mask < wide_count:
            value = value.reshape((-1, 2) + value.shape[1:])
            sent = lax.ppermute(
                value[:, 1].astype(jnp.bfloat16),
                "wide",
                [(i, i ^ mask) for i in range(wide_count)],
            )
            value = value[:, 0] + sent.astype(jnp.float32)
            mask *= 2
        results.append(value[0])
    return jnp.stack(results)


def solution(mesh):
    in_specs = (
        P(("wide", "narrow"), None, None, None),
        P(("wide", "narrow"), None),
        P(("wide", "narrow"), None),
        P(("wide", "narrow")),
        P(("wide", "narrow")),
        P("wide", None, None),
        P("wide"),
        P("wide", None),
        P("wide", None),
        P("wide", None),
        P("wide", None),
        P("narrow", None),
    )
    out_specs = P(None, "wide", "narrow")

    return jax.shard_map(body, mesh=mesh, in_specs=in_specs, out_specs=out_specs, check_vma=False)
```

profile of v0, /device:TPU:0, one launch (start us, length us, event | category | flops | bytes accessed | tf_op | source)
XLA Modules:
  0.0 276.3 jit_solution(12888081649662713137)
XLA Ops:
  1.1 7.8 %all_to_all.19 = s32[4,1,64]{2,1,0:T(1,128)S(1)} all-to-all(s32[4,1,64]{2,1,0:T(1,128)S(1)} %broadcast_in_dim.43), channel_id=1, replica_groups=mesh['wide'=8,'narrow'=4] {'narrow'}, dimensions={0} | all-to-all | bytes 2048 | tf_op jit(solution)/shard_map/all_to_all | solution.py:264
  9.0 4.4 %collective-permute-start.4 = (bf16[640,640]{1,0:T(8,128)(2,1)S(1)}, bf16[640,640]{1,0:T(8,128)(2,1)}, u32[]{:S(2)}, u32[]{:S(2)}) collective-permute-start(bf16[640,640]{1,0:T(8,128)(2,1)S(1)} %dynamic-slice_bitcast_fusion.refs_0_), channel_id=1, source_target_pairs={{0,8},{4,12},{8,16},{12,20},{16,24},{20,28},{1,9},{5,13},{9,17},{1... | collective-permute-start | bytes 2457608 | tf_op jit(solution)/shard_map/ppermute | solution.py:230
  13.4 1.3 collective-permute-start.6
  14.7 1.6 collective-permute-start
  16.3 0.9 copy-done.6
  17.2 12.7 %collective-permute-done.4.refs_0_.refs_2_ = bf16[640,640]{1,0:T(8,128)(2,1)} collective-permute-done((bf16[640,640]{1,0:T(8,128)(2,1)S(1)}, bf16[640,640]{1,0:T(8,128)(2,1)}, u32[]{:S(2)}, u32[]{:S(2)}) %collective-permute-start.4) | collective-permute-done | bytes 819232 | tf_op jit(solution)/shard_map/ppermute | solution.py:230
  29.9 1.5 collective-permute-start.8
  31.5 3.5 %collective-permute-done.6.refs_2_.refs_4_ = bf16[640,640]{1,0:T(8,128)(2,1)S(1)} collective-permute-done((bf16[640,640]{1,0:T(8,128)(2,1)S(1)}, bf16[640,640]{1,0:T(8,128)(2,1)S(1)}, u32[]{:S(2)}, u32[]{:S(2)}) %collective-permute-start.6) | collective-permute-done | bytes 819232 | tf_op jit(solution)/shard_map/ppermute | solution.py:235
  34.9 1.3 collective-permute-start.10
  36.2 9.1 %collective-permute-done.2.refs_4_.refs_6_ = bf16[16,384,128]{2,1,0:T(8,128)(2,1)} collective-permute-done((bf16[16,384,128]{2,1,0:T(8,128)(2,1)}, bf16[16,384,128]{2,1,0:T(8,128)(2,1)}, u32[]{:S(2)}, u32[]{:S(2)}) %collective-permute-start.2) | collective-permute-done | bytes 1572896 | tf_op jit(solution)/shard_map/ppermute | solution.py:240
  47.6 1.6 collective-permute-start.5
  49.2 1.6 collective-permute-start.12
  50.8 5.2 %collective-permute-done.10.refs_2_.refs_8_ = bf16[640,640]{1,0:T(8,128)(2,1)} collective-permute-done((bf16[640,640]{1,0:T(8,128)(2,1)S(1)}, bf16[640,640]{1,0:T(8,128)(2,1)}, u32[]{:S(2)}, u32[]{:S(2)}) %collective-permute-start.10) | collective-permute-done | bytes 819232 | tf_op jit(solution)/shard_map/ppermute | solution.py:235
  56.0 1.3 collective-permute-start.14
  57.3 3.6 %gather_fusion.1 = bf16[16,128,512]{2,1,0:T(8,128)(2,1)} fusion(bf16[16,128,512]{2,1,0:T(8,128)(2,1)} %bitcast.149, s32[1024]{0:T(1024)S(1)} %pad_clamp_fusion.1), kind=kCustom, calls=%fused_computation.1 | custom fusion | bytes 4194368 | tf_op jit(solution)/shard_map/gather | solution.py:289
  60.9 3.9 %copy.34 = bf16[16,128,512]{1,2,0:T(8,128)(2,1)} copy(bf16[16,128,512]{2,1,0:T(8,128)(2,1)} %gather_fusion.1) | data formatting | bytes 4194304 | tf_op jit(solution)/shard_map/gather | solution.py:289
  64.9 6.2 %gather_fusion.2 = bf16[16,128,1024]{2,1,0:T(8,128)(2,1)} fusion(bf16[32,128,1024]{2,1,0:T(8,128)(2,1)} %bitcast.148, s32[1024]{0:T(1024)S(1)} %pad_clamp_fusion), kind=kCustom, calls=%fused_computation.2 | custom fusion | bytes 8388672 | tf_op jit(solution)/shard_map/gather | solution.py:290
  71.8 3.4 %collective-permute-start.7 = (bf16[640,640]{1,0:T(8,128)(2,1)}, bf16[640,640]{1,0:T(8,128)(2,1)}, u32[]{:S(2)}, u32[]{:S(2)}) collective-permute-start(bf16[640,640]{1,0:T(8,128)(2,1)} %copy-done.13), channel_id=1, source_target_pairs={{0,4},{4,0},{8,12},{12,8},{16,20},{20,16},{1,5},{5,1},{9,13},{13,9... | collective-permute-start | bytes 2457608 | tf_op jit(solution)/shard_map/ppermute | solution.py:227
  75.2 1.6 collective-permute-start.9
  76.8 2.4 collective-permute-start.11
  79.2 1.6 collective-permute-start.13
  80.8 1.2 copy-done.3
  82.0 3.4 %collective-permute-start.15 = (bf16[640,640]{1,0:T(8,128)(2,1)}, bf16[640,640]{1,0:T(8,128)(2,1)}, u32[]{:S(2)}, u32[]{:S(2)}) collective-permute-start(bf16[640,640]{1,0:T(8,128)(2,1)} %collective-permute-done.14.refs_2_.refs_12_), channel_id=1, source_target_pairs={{0,4},{4,0},{1,5},{5,1},{2,6},{6,2},{3,7},{7,3}} | collective-permute-start | bytes 2457608 | tf_op jit(solution)/shard_map/ppermute | solution.py:227
  85.9 1.4 copy-done.2
  87.3 1.4 copy-done.4
  88.7 1.1 copy-done.7
  89.9 1.1 copy-done.11
  91.0 7.8 %density.4 = f32[8,3,640]{2,1,0:T(4,128)S(1)} custom-call(s32[128]{0:T(128)S(1)} %get-tuple-element.71.slot_ref, s32[128]{0:T(128)S(1)} %reshape_squeeze.4.dest_ref, s32[128]{0:T(128)S(1)} %get-tuple-element.85.row_ref, s32[128]{0:T(128)S(1)} %get-tuple-element.88.col_ref, bf16[640,640]{1,0:T(8,128)(2,1)S(1)} %copy-done.7, bf16[640,640]{1,0:T(8,128)(2,1)S(1)} %copy-done.11, ...), custom_call_target="tpu_custom_call" | custom-call | flops 1000000000 | bytes 10000000 | tf_op jit(solution)/shard_map/density/pallas_call | solution.py:61
  98.8 8.3 %density.5 = f32[8,3,640]{2,1,0:T(4,128)S(1)} custom-call(s32[128]{0:T(128)S(1)} %get-tuple-element.42.slot_ref, s32[128]{0:T(128)S(1)} %reshape_squeeze.4.dest_ref, s32[128]{0:T(128)S(1)} %get-tuple-element.85.row_ref, s32[128]{0:T(128)S(1)} %get-tuple-element.88.col_ref, bf16[640,640]{1,0:T(8,128)(2,1)} %collective-permute-done.4.refs_0_.refs_2_, ...), custom_call_target="tpu_custom_call" | custom-call | flops 1000000000 | bytes 10000000 | tf_op jit(solution)/shard_map/density/pallas_call | solution.py:61
  107.2 5.5 %collective-permute-done.11.refs_3_.refs_9_ = bf16[640,640]{1,0:T(8,128)(2,1)} collective-permute-done((bf16[640,640]{1,0:T(8,128)(2,1)}, bf16[640,640]{1,0:T(8,128)(2,1)}, u32[]{:S(2)}, u32[]{:S(2)}) %collective-permute-start.11) | collective-permute-done | bytes 819232 | tf_op jit(solution)/shard_map/ppermute | solution.py:227
  112.7 10.2 %density.6 = f32[8,3,640]{2,1,0:T(4,128)S(1)} custom-call(s32[128]{0:T(128)S(1)} %get-tuple-element.44.slot_ref, s32[128]{0:T(128)S(1)} %reshape_squeeze.4.dest_ref, s32[128]{0:T(128)S(1)} %get-tuple-element.85.row_ref, s32[128]{0:T(128)S(1)} %get-tuple-element.88.col_ref, bf16[640,640]{1,0:T(8,128)(2,1)} %collective-permute-done.8.refs_0_.refs_6_, ...), custom_call_target="tpu_custom_call" | custom-call | flops 1000000000 | bytes 10000000 | tf_op jit(solution)/shard_map/density/pallas_call | solution.py:61
  123.0 4.3 %collective-permute-done.15.refs_3_.refs_13_ = bf16[640,640]{1,0:T(8,128)(2,1)} collective-permute-done((bf16[640,640]{1,0:T(8,128)(2,1)}, bf16[640,640]{1,0:T(8,128)(2,1)}, u32[]{:S(2)}, u32[]{:S(2)}) %collective-permute-start.15) | collective-permute-done | bytes 819232 | tf_op jit(solution)/shard_map/ppermute | solution.py:227
  127.3 7.6 %density.7 = f32[8,3,640]{2,1,0:T(4,128)S(1)} custom-call(s32[128]{0:T(128)S(1)} %get-tuple-element.46.slot_ref, s32[128]{0:T(128)S(1)} %reshape_squeeze.4.dest_ref, s32[128]{0:T(128)S(1)} %get-tuple-element.85.row_ref, s32[128]{0:T(128)S(1)} %get-tuple-element.88.col_ref, bf16[640,640]{1,0:T(8,128)(2,1)} %collective-permute-done.12.refs_0_.refs_10_, ...), custom_call_target="tpu_custom_call" | custom-call | flops 1000000000 | bytes 10000000 | tf_op jit(solution)/shard_map/density/pallas_call | solution.py:61
  135.6 4.0 %all-to-all-start.1 = ((f32[8,3,640]{2,1,0:T(4,128)}), f32[8,3,640]{2,1,0:T(4,128)S(1)}, u32[]{:S(2)}, u32[]{:S(2)}) async-start(f32[8,3,640]{2,1,0:T(4,128)} %add.192), calls=%async_computation.1 | async-start | bytes 163840 | tf_op jit(solution)/shard_map/all_to_all | solution.py:300
  141.0 1.5 fusion.29
  142.5 4.1 %all-to-all-done.1 = f32[8,3,640]{2,1,0:T(4,128)S(1)} async-done(((f32[8,3,640]{2,1,0:T(4,128)}), f32[8,3,640]{2,1,0:T(4,128)S(1)}, u32[]{:S(2)}, u32[]{:S(2)}) %all-to-all-start.1) | async-done | bytes 61472 | tf_op jit(solution)/shard_map/all_to_all | solution.py:300
  147.3 3.4 %all-to-all-start.2 = ((f32[8,3,640]{2,1,0:T(4,128)}), f32[8,3,640]{2,1,0:T(4,128)S(1)}, u32[]{:S(2)}, u32[]{:S(2)}) async-start(f32[8,3,640]{2,1,0:T(4,128)} %broadcast_in_dim.48), calls=%async_computation.2 | async-start | bytes 163840 | tf_op jit(solution)/shard_map/all_to_all | solution.py:312
  150.8 6.8 %all-to-all-done.2.pot_ref = f32[8,3,640]{2,1,0:T(4,128)S(1)} async-done(((f32[8,3,640]{2,1,0:T(4,128)}), f32[8,3,640]{2,1,0:T(4,128)S(1)}, u32[]{:S(2)}, u32[]{:S(2)}) %all-to-all-start.2) | async-done | bytes 61472 | tf_op jit(solution)/shard_map/all_to_all | solution.py:312
  157.6 1.1 copy-done.8
  158.7 1.1 copy-done.12
  159.9 1.1 copy-done.15
  161.0 11.5 %blocks.2 = (bf16[16,128,128]{2,1,0:T(8,128)(2,1)S(1)}, bf16[16,128,128]{2,1,0:T(8,128)(2,1)S(1)}, bf16[16,128,128]{2,1,0:T(8,128)(2,1)S(1)}, bf16[16,128,128]{2...) custom-call(s32[14]{0:T(128)S(1)} %stack.82.place_ref, ...), custom_call_target="tpu_custom_call" | custom-call | flops 4000000000 | bytes 10000000 | tf_op jit(solution)/shard_map/blocks/pallas_call | solution.py:127
  173.2 1.3 collective-permute-done.16
  176.2 15.5 %blocks.3 = (bf16[16,128,128]{2,1,0:T(8,128)(2,1)S(1)}, bf16[16,128,128]{2,1,0:T(8,128)(2,1)S(1)}, bf16[16,128,128]{2,1,0:T(8,128)(2,1)S(1)}, bf16[16,128,128]{2...) custom-call(s32[14]{0:T(128)S(1)} %stack.82.place_ref, ...), custom_call_target="tpu_custom_call" | custom-call | flops 4000000000 | bytes 10000000 | tf_op jit(solution)/shard_map/blocks/pallas_call | solution.py:127
  191.9 7.6 %collective-permute-start.34 = (bf16[16,128,128]{2,1,0:T(8,128)(2,1)S(1)}, bf16[16,128,128]{2,1,0:T(8,128)(2,1)S(1)}, u32[]{:S(2)}, u32[]{:S(2)}) collective-permute-start(bf16[16,128,128]{2,1,0:T(8,128)(2,1)S(1)} %add_convert_fusion.3), channel_id=1, source_target_pairs={{0,2},{1,3},{2,0},{3,1},{4,6},{5,7},{6,4},{7,5},{8,10},{9,11},{10,... | collective-permute-start | bytes 1572872 | tf_op jit(solution)/shard_map/ppermute | solution.py:240
  200.1 1.7 collective-permute-start.20
  201.9 10.3 %collective-permute-done.34.refs_1_ = bf16[16,128,128]{2,1,0:T(8,128)(2,1)S(1)} collective-permute-done((bf16[16,128,128]{2,1,0:T(8,128)(2,1)S(1)}, bf16[16,128,128]{2,1,0:T(8,128)(2,1)S(1)}, u32[]{:S(2)}, u32[]{:S(2)}) %collective-permute-start.34) | collective-permute-done | bytes 524320 | tf_op jit(solution)/shard_map/ppermute | solution.py:240
  212.2 6.0 %project.5 = (f32[2,512,256]{2,1,0:T(8,128)S(1)}, bf16[2,512,256]{2,1,0:T(8,128)(2,1)S(1)}) custom-call(s32[10]{0:T(128)S(1)} %pad_add_fusion.1.where_ref, bf16[16,128,128]{2,1,0:T(8,128)(2,1)S(1)} %add_convert_fusion.refs_0_, bf16[16,128,128]{2,1,0:T(8,128)(2,1)S(1)} %collective-permute-done.34.refs_1_, bf16[16,512,128]{2,1,0:T(8,128)(2,1)S(1)} %bitcast.145, ...), custom_call_target="tpu_custom_call" | custom-call | flops 2400000000 | bytes 10000000 | tf_op jit(solution)/shard_map/project/pallas_call | solution.py:182
  218.5 5.0 %collective-permute-done.27.refs_1_ = bf16[16,128,128]{2,1,0:T(8,128)(2,1)S(1)} collective-permute-done((bf16[16,128,128]{2,1,0:T(8,128)(2,1)S(1)}, bf16[16,128,128]{2,1,0:T(8,128)(2,1)S(1)}, u32[]{:S(2)}, u32[]{:S(2)}) %collective-permute-start.27) | collective-permute-done | bytes 524320 | tf_op jit(solution)/shard_map/ppermute | solution.py:240
  223.4 6.0 %project.4 = (f32[2,512,256]{2,1,0:T(8,128)S(1)}, bf16[2,512,256]{2,1,0:T(8,128)(2,1)S(1)}) custom-call(s32[10]{0:T(128)S(1)} %pad_add_fusion.1.where_ref, bf16[16,128,128]{2,1,0:T(8,128)(2,1)S(1)} %add_convert_fusion.1.refs_0_, bf16[16,128,128]{2,1,0:T(8,128)(2,1)S(1)} %collective-permute-done.27.refs_1_, bf16[16,512,128]{2,1,0:T(8,128)(2,1)S(1)} %bitcast.146, ...), custom_call_target="tpu_custom_call" | custom-call | flops 2400000000 | bytes 10000000 | tf_op jit(solution)/shard_map/project/pallas_call | solution.py:182
  229.7 4.7 %collective-permute-done.20.refs_1_ = bf16[16,128,128]{2,1,0:T(8,128)(2,1)S(1)} collective-permute-done((bf16[16,128,128]{2,1,0:T(8,128)(2,1)S(1)}, bf16[16,128,128]{2,1,0:T(8,128)(2,1)S(1)}, u32[]{:S(2)}, u32[]{:S(2)}) %collective-permute-start.20) | collective-permute-done | bytes 524320 | tf_op jit(solution)/shard_map/ppermute | solution.py:240
  234.4 6.0 %project.3 = (f32[2,512,256]{2,1,0:T(8,128)S(1)}, bf16[2,512,256]{2,1,0:T(8,128)(2,1)S(1)}) custom-call(s32[10]{0:T(128)S(1)} %pad_add_fusion.1.where_ref, bf16[16,128,128]{2,1,0:T(8,128)(2,1)S(1)} %add_convert_fusion.2.refs_0_, bf16[16,128,128]{2,1,0:T(8,128)(2,1)S(1)} %collective-permute-done.20.refs_1_, bf16[16,512,128]{2,1,0:T(8,128)(2,1)S(1)} %bitcast.147, ...), custom_call_target="tpu_custom_call" | custom-call | flops 2400000000 | bytes 10000000 | tf_op jit(solution)/shard_map/project/pallas_call | solution.py:182
  240.6 1.8 collective-permute-start.36
  243.1 1.8 collective-permute-start.22
  244.9 5.0 %collective-permute-done.36 = bf16[1,512,256]{2,1,0:T(8,128)(2,1)S(1)} collective-permute-done((bf16[1,512,256]{2,1,0:T(8,128)(2,1)S(1)}, bf16[1,512,256]{2,1,0:T(8,128)(2,1)S(1)}, u32[]{:S(2)}, u32[]{:S(2)}) %collective-permute-start.36) | collective-permute-done | bytes 262176 | tf_op jit(solution)/shard_map/ppermute | solution.py:240
  250.0 5.5 %collective-permute-done.29 = bf16[1,512,256]{2,1,0:T(8,128)(2,1)S(1)} collective-permute-done((bf16[1,512,256]{2,1,0:T(8,128)(2,1)S(1)}, bf16[1,512,256]{2,1,0:T(8,128)(2,1)S(1)}, u32[]{:S(2)}, u32[]{:S(2)}) %collective-permute-start.29) | collective-permute-done | bytes 262176 | tf_op jit(solution)/shard_map/ppermute | solution.py:240
  255.6 5.0 %collective-permute-done.22 = bf16[1,512,256]{2,1,0:T(8,128)(2,1)S(1)} collective-permute-done((bf16[1,512,256]{2,1,0:T(8,128)(2,1)S(1)}, bf16[1,512,256]{2,1,0:T(8,128)(2,1)S(1)}, u32[]{:S(2)}, u32[]{:S(2)}) %collective-permute-start.22) | collective-permute-done | bytes 262176 | tf_op jit(solution)/shard_map/ppermute | solution.py:240
  261.0 2.1 collective-permute-start.31
  263.1 2.8 collective-permute-done.23
  266.0 1.2 collective-permute-start.39
  267.3 1.8 collective-permute-start.32
  269.1 1.2 collective-permute-done.24
  270.9 2.3 collective-permute-done.32
  273.2 2.4 collective-permute-done.25
  (140 shorter events, 14.2 us)
Async XLA Ops:
  0.0 8.9 %copy-start = (bf16[2,640,1280]{2,1,0:T(8,128)(2,1)S(1)}, bf16[2,640,1280]{2,1,0:T(8,128)(2,1)}, u32[]{:S(2)}) copy-start(bf16[2,640,1280]{2,1,0:T(8,128)(2,1)} %param.17) | copy-start | bytes 9830404
  8.9 36.4 %collective-permute-start.2 = (bf16[16,384,128]{2,1,0:T(8,128)(2,1)}, bf16[16,384,128]{2,1,0:T(8,128)(2,1)}, u32[]{:S(2)}, u32[]{:S(2)}) collective-permute-start(bf16[16,384,128]{2,1,0:T(8,128)(2,1)} %bitcast.136), channel_id=1, source_target_pairs={{0,2},{1,3},{2,0},{3,1},{4,6},{5,7},{6,4},{7,5},{8,10},{9,11},{10,... | collective-permute-start | bytes 4718600 | tf_op jit(solution)/shard_map/ppermute | solution.py:240
  9.0 21.0 %collective-permute-start.4 = (bf16[640,640]{1,0:T(8,128)(2,1)S(1)}, bf16[640,640]{1,0:T(8,128)(2,1)}, u32[]{:S(2)}, u32[]{:S(2)}) collective-permute-start(bf16[640,640]{1,0:T(8,128)(2,1)S(1)} %dynamic-slice_bitcast_fusion.refs_0_), channel_id=1, source_target_pairs={{0,8},{4,12},{8,16},{12,20},{16,24},{20,28},{1,9},{5,13},{9,17},{1... | collective-permute-start | bytes 2457608 | tf_op jit(solution)/shard_map/ppermute | solution.py:230
  13.4 21.6 %collective-permute-start.6 = (bf16[640,640]{1,0:T(8,128)(2,1)S(1)}, bf16[640,640]{1,0:T(8,128)(2,1)S(1)}, u32[]{:S(2)}, u32[]{:S(2)}) collective-permute-start(bf16[640,640]{1,0:T(8,128)(2,1)S(1)} %dynamic-slice_bitcast_fusion.refs_0_), channel_id=1, source_target_pairs={{8,0},{12,4},{16,8},{20,12},{24,16},{28,20},{9,1},{13,5},{17,9},{2... | collective-permute-start | bytes 2457608 | tf_op jit(solution)/shard_map/ppermute | solution.py:235
  14.7 57.1 %collective-permute-start.1 = (bf16[16,384,128]{2,1,0:T(8,128)(2,1)}, bf16[16,384,128]{2,1,0:T(8,128)(2,1)S(1)}, u32[]{:S(2)}, u32[]{:S(2)}) collective-permute-start(bf16[16,384,128]{2,1,0:T(8,128)(2,1)} %bitcast.137), channel_id=1, source_target_pairs={{0,1},{1,0},{2,3},{3,2},{4,5},{5,4},{6,7},{7,6},{8,9},{9,8},{10,11... | collective-permute-start | bytes 4718600 | tf_op jit(solution)/shard_map/ppermute | solution.py:240
  14.7 31.9 %collective-permute-start = (bf16[640,640]{1,0:T(8,128)(2,1)S(1)}, bf16[640,640]{1,0:T(8,128)(2,1)S(1)}, u32[]{:S(2)}, u32[]{:S(2)}) collective-permute-start(bf16[640,640]{1,0:T(8,128)(2,1)S(1)} %dynamic-slice_bitcast_fusion.refs_0_), channel_id=1, source_target_pairs={{0,4},{4,0},{8,12},{12,8},{16,20},{20,16},{24,28},{28,24},{1,5},{5... | collective-permute-start | bytes 2457608 | tf_op jit(solution)/shard_map/ppermute | solution.py:227
  16.3 0.9 copy-start.6
  29.9 19.3 %collective-permute-start.8 = (bf16[640,640]{1,0:T(8,128)(2,1)}, bf16[640,640]{1,0:T(8,128)(2,1)}, u32[]{:S(2)}, u32[]{:S(2)}) collective-permute-start(bf16[640,640]{1,0:T(8,128)(2,1)} %collective-permute-done.4.refs_0_.refs_2_), channel_id=1, source_target_pairs={{8,16},{12,20},{16,24},{20,28},{9,17},{13,21},{17,25},{21,29},{10,... | collective-permute-start | bytes 2457608 | tf_op jit(solution)/shard_map/ppermute | solution.py:230
  34.9 11.7 %copy-start.13 = (bf16[640,640]{1,0:T(8,128)(2,1)}, bf16[640,640]{1,0:T(8,128)(2,1)S(1)}, u32[]{:S(2)}) copy-start(bf16[640,640]{1,0:T(8,128)(2,1)S(1)} %collective-permute-done.6.refs_2_.refs_4_) | copy-start | bytes 2457604
  34.9 21.0 %collective-permute-start.10 = (bf16[640,640]{1,0:T(8,128)(2,1)S(1)}, bf16[640,640]{1,0:T(8,128)(2,1)}, u32[]{:S(2)}, u32[]{:S(2)}) collective-permute-start(bf16[640,640]{1,0:T(8,128)(2,1)S(1)} %collective-permute-done.6.refs_2_.refs_4_), channel_id=1, source_target_pairs={{8,0},{12,4},{16,8},{20,12},{9,1},{13,5},{17,9},{21,13},{10,2},{14... | collective-permute-start | bytes 2457608 | tf_op jit(solution)/shard_map/ppermute | solution.py:235
  45.3 35.5 %collective-permute-start.3 = (bf16[16,384,128]{2,1,0:T(8,128)(2,1)}, bf16[16,384,128]{2,1,0:T(8,128)(2,1)S(1)}, u32[]{:S(2)}, u32[]{:S(2)}) collective-permute-start(bf16[16,384,128]{2,1,0:T(8,128)(2,1)} %collective-permute-done.2.refs_4_.refs_6_), channel_id=1, source_target_pairs={{0,1},{1,0},{2,3},{3,2},{4,5},{5,4},{6,7},{7,6},{8,9},{9,8},{10,11... | collective-permute-start | bytes 4718600 | tf_op jit(solution)/shard_map/ppermute | solution.py:240
  46.7 0.9 copy-start.10
  47.6 27.6 %collective-permute-start.5 = (bf16[640,640]{1,0:T(8,128)(2,1)}, bf16[640,640]{1,0:T(8,128)(2,1)}, u32[]{:S(2)}, u32[]{:S(2)}) collective-permute-start(bf16[640,640]{1,0:T(8,128)(2,1)} %collective-permute-done.4.refs_0_.refs_2_), channel_id=1, source_target_pairs={{8,12},{12,8},{16,20},{20,16},{24,28},{28,24},{9,13},{13,9},{17,21... | collective-permute-start | bytes 2457608 | tf_op jit(solution)/shard_map/ppermute | solution.py:227
  49.2 27.6 %collective-permute-start.12 = (bf16[640,640]{1,0:T(8,128)(2,1)}, bf16[640,640]{1,0:T(8,128)(2,1)}, u32[]{:S(2)}, u32[]{:S(2)}) collective-permute-start(bf16[640,640]{1,0:T(8,128)(2,1)} %collective-permute-done.8.refs_0_.refs_6_), channel_id=1, source_target_pairs={{16,24},{20,28},{17,25},{21,29},{18,26},{22,30},{19,27},{23,31}} | collective-permute-start | bytes 2457608 | tf_op jit(solution)/shard_map/ppermute | solution.py:230
  56.0 23.2 %collective-permute-start.14 = (bf16[640,640]{1,0:T(8,128)(2,1)}, bf16[640,640]{1,0:T(8,128)(2,1)}, u32[]{:S(2)}, u32[]{:S(2)}) collective-permute-start(bf16[640,640]{1,0:T(8,128)(2,1)} %collective-permute-done.10.refs_2_.refs_8_), channel_id=1, source_target_pairs={{8,0},{12,4},{9,1},{13,5},{10,2},{14,6},{11,3},{15,7}} | collective-permute-start | bytes 2457608 | tf_op jit(solution)/shard_map/ppermute | solution.py:235
  71.8 27.0 %collective-permute-start.7 = (bf16[640,640]{1,0:T(8,128)(2,1)}, bf16[640,640]{1,0:T(8,128)(2,1)}, u32[]{:S(2)}, u32[]{:S(2)}) collective-permute-start(bf16[640,640]{1,0:T(8,128)(2,1)} %copy-done.13), channel_id=1, source_target_pairs={{0,4},{4,0},{8,12},{12,8},{16,20},{20,16},{1,5},{5,1},{9,13},{13,9... | collective-permute-start | bytes 2457608 | tf_op jit(solution)/shard_map/ppermute | solution.py:227
  75.2 31.9 %collective-permute-start.9 = (bf16[640,640]{1,0:T(8,128)(2,1)}, bf16[640,640]{1,0:T(8,128)(2,1)}, u32[]{:S(2)}, u32[]{:S(2)}) collective-permute-start(bf16[640,640]{1,0:T(8,128)(2,1)} %collective-permute-done.8.refs_0_.refs_6_), channel_id=1, source_target_pairs={{16,20},{20,16},{24,28},{28,24},{17,21},{21,17},{25,29},{29,25},{1... | collective-permute-start | bytes 2457608 | tf_op jit(solution)/shard_map/ppermute | solution.py:227
  76.8 35.9 %collective-permute-start.11 = (bf16[640,640]{1,0:T(8,128)(2,1)}, bf16[640,640]{1,0:T(8,128)(2,1)}, u32[]{:S(2)}, u32[]{:S(2)}) collective-permute-start(bf16[640,640]{1,0:T(8,128)(2,1)} %collective-permute-done.10.refs_2_.refs_8_), channel_id=1, source_target_pairs={{0,4},{4,0},{8,12},{12,8},{1,5},{5,1},{9,13},{13,9},{2,6},{6,2},{1... | collective-permute-start | bytes 2457608 | tf_op jit(solution)/shard_map/ppermute | solution.py:227
  79.2 43.7 %collective-permute-start.13 = (bf16[640,640]{1,0:T(8,128)(2,1)}, bf16[640,640]{1,0:T(8,128)(2,1)}, u32[]{:S(2)}, u32[]{:S(2)}) collective-permute-start(bf16[640,640]{1,0:T(8,128)(2,1)} %collective-permute-done.12.refs_0_.refs_10_), channel_id=1, source_target_pairs={{24,28},{28,24},{25,29},{29,25},{26,30},{30,26},{27,31},{31,27}} | collective-permute-start | bytes 2457608 | tf_op jit(solution)/shard_map/ppermute | solution.py:227
  80.8 1.2 copy-start.3
  82.0 45.3 %collective-permute-start.15 = (bf16[640,640]{1,0:T(8,128)(2,1)}, bf16[640,640]{1,0:T(8,128)(2,1)}, u32[]{:S(2)}, u32[]{:S(2)}) collective-permute-start(bf16[640,640]{1,0:T(8,128)(2,1)} %collective-permute-done.14.refs_2_.refs_12_), channel_id=1, source_target_pairs={{0,4},{4,0},{1,5},{5,1},{2,6},{6,2},{3,7},{7,3}} | collective-permute-start | bytes 2457608 | tf_op jit(solution)/shard_map/ppermute | solution.py:227
  85.9 1.4 copy-start.2
  87.3 1.4 copy-start.4
  88.7 1.1 copy-start.7
  89.9 1.1 copy-start.11
  91.0 7.8 %copy-start.14 = (bf16[640,640]{1,0:T(8,128)(2,1)S(1)}, bf16[640,640]{1,0:T(8,128)(2,1)}, u32[]{:S(2)}) copy-start(bf16[640,640]{1,0:T(8,128)(2,1)} %copy-done.13) | copy-start | bytes 2457604
  122.9 16.6 %copy-start.17 = (s32[2]{0:T(128)S(1)}, s32[2]{0:T(128)}, u32[]{:S(2)}) copy-start(s32[2]{0:T(128)} %param.18) | copy-start | bytes 28
  135.6 11.0 %all-to-all-start.1 = ((f32[8,3,640]{2,1,0:T(4,128)}), f32[8,3,640]{2,1,0:T(4,128)S(1)}, u32[]{:S(2)}, u32[]{:S(2)}) async-start(f32[8,3,640]{2,1,0:T(4,128)} %add.192), calls=%async_computation.1 | async-start | bytes 163840 | tf_op jit(solution)/shard_map/all_to_all | solution.py:300
  147.3 10.3 %all-to-all-start.2 = ((f32[8,3,640]{2,1,0:T(4,128)}), f32[8,3,640]{2,1,0:T(4,128)S(1)}, u32[]{:S(2)}, u32[]{:S(2)}) async-start(f32[8,3,640]{2,1,0:T(4,128)} %broadcast_in_dim.48), calls=%async_computation.2 | async-start | bytes 163840 | tf_op jit(solution)/shard_map/all_to_all | solution.py:312
  157.6 1.1 copy-start.8
  158.7 1.1 copy-start.12
  159.9 1.1 copy-start.15
  172.5 2.0 collective-permute-start.16
  172.6 2.6 collective-permute-start.17
  173.1 2.9 %collective-permute-start.18 = (bf16[16,128,128]{2,1,0:T(8,128)(2,1)S(1)}, bf16[16,128,128]{2,1,0:T(8,128)(2,1)S(1)}, u32[]{:S(2)}, u32[]{:S(2)}) collective-permute-start(bf16[16,128,128]{2,1,0:T(8,128)(2,1)S(1)} %get-tuple-element.52), channel_id=1, source_target_pairs={{0,1},{1,0},{2,3},{3,2},{4,5},{5,4},{6,7},{7,6},{8,9},{9,8},{10,11... | collective-permute-start | bytes 1572872 | tf_op jit(solution)/shard_map/ppermute | solution.py:240
  174.5 1.7 copy-start.16
  176.2 36.1 %copy-start.5 = (bf16[16,128,1024]{2,1,0:T(8,128)(2,1)S(1)}, bf16[16,128,1024]{2,1,0:T(8,128)(2,1)}, u32[]{:S(2)}) copy-start(bf16[16,128,1024]{2,1,0:T(8,128)(2,1)} %gather_fusion.2) | copy-start | bytes 12582916
  176.2 36.0 %copy-start.9 = (bf16[16,128,512]{1,2,0:T(8,128)(2,1)S(1)}, bf16[16,128,512]{1,2,0:T(8,128)(2,1)}, u32[]{:S(2)}) copy-start(bf16[16,128,512]{1,2,0:T(8,128)(2,1)} %copy.34) | copy-start | bytes 6291460
  191.6 8.5 %collective-permute-start.33 = (bf16[16,128,128]{2,1,0:T(8,128)(2,1)S(1)}, bf16[16,128,128]{2,1,0:T(8,128)(2,1)S(1)}, u32[]{:S(2)}, u32[]{:S(2)}) collective-permute-start(bf16[16,128,128]{2,1,0:T(8,128)(2,1)S(1)} %get-tuple-element.67), channel_id=1, source_target_pairs={{0,1},{1,0},{2,3},{3,2},{4,5},{5,4},{6,7},{7,6},{8,9},{9,8},{10,11... | collective-permute-start | bytes 1572872 | tf_op jit(solution)/shard_map/ppermute | solution.py:240
  191.9 20.3 %collective-permute-start.34 = (bf16[16,128,128]{2,1,0:T(8,128)(2,1)S(1)}, bf16[16,128,128]{2,1,0:T(8,128)(2,1)S(1)}, u32[]{:S(2)}, u32[]{:S(2)}) collective-permute-start(bf16[16,128,128]{2,1,0:T(8,128)(2,1)S(1)} %add_convert_fusion.3), channel_id=1, source_target_pairs={{0,2},{1,3},{2,0},{3,1},{4,6},{5,7},{6,4},{7,5},{8,10},{9,11},{10,... | collective-permute-start | bytes 1572872 | tf_op jit(solution)/shard_map/ppermute | solution.py:240
  199.4 18.9 %collective-permute-start.26 = (bf16[16,128,128]{2,1,0:T(8,128)(2,1)S(1)}, bf16[16,128,128]{2,1,0:T(8,128)(2,1)S(1)}, u32[]{:S(2)}, u32[]{:S(2)}) collective-permute-start(bf16[16,128,128]{2,1,0:T(8,128)(2,1)S(1)} %get-tuple-element.62), channel_id=1, source_target_pairs={{0,1},{1,0},{2,3},{3,2},{4,5},{5,4},{6,7},{7,6},{8,9},{9,8},{10,11... | collective-permute-start | bytes 1572872 | tf_op jit(solution)/shard_map/ppermute | solution.py:240
  199.6 23.8 %collective-permute-start.27 = (bf16[16,128,128]{2,1,0:T(8,128)(2,1)S(1)}, bf16[16,128,128]{2,1,0:T(8,128)(2,1)S(1)}, u32[]{:S(2)}, u32[]{:S(2)}) collective-permute-start(bf16[16,128,128]{2,1,0:T(8,128)(2,1)S(1)} %add_convert_fusion.4), channel_id=1, source_target_pairs={{0,2},{1,3},{2,0},{3,1},{4,6},{5,7},{6,4},{7,5},{8,10},{9,11},{10,... | collective-permute-start | bytes 1572872 | tf_op jit(solution)/shard_map/ppermute | solution.py:240
  199.9 29.6 %collective-permute-start.19 = (bf16[16,128,128]{2,1,0:T(8,128)(2,1)S(1)}, bf16[16,128,128]{2,1,0:T(8,128)(2,1)S(1)}, u32[]{:S(2)}, u32[]{:S(2)}) collective-permute-start(bf16[16,128,128]{2,1,0:T(8,128)(2,1)S(1)} %get-tuple-element.55), channel_id=1, source_target_pairs={{0,1},{1,0},{2,3},{3,2},{4,5},{5,4},{6,7},{7,6},{8,9},{9,8},{10,11... | collective-permute-start | bytes 1572872 | tf_op jit(solution)/shard_map/ppermute | solution.py:240
  200.1 34.3 %collective-permute-start.20 = (bf16[16,128,128]{2,1,0:T(8,128)(2,1)S(1)}, bf16[16,128,128]{2,1,0:T(8,128)(2,1)S(1)}, u32[]{:S(2)}, u32[]{:S(2)}) collective-permute-start(bf16[16,128,128]{2,1,0:T(8,128)(2,1)S(1)} %add_convert_fusion.5), channel_id=1, source_target_pairs={{0,2},{1,3},{2,0},{3,1},{4,6},{5,7},{6,4},{7,5},{8,10},{9,11},{10,... | collective-permute-start | bytes 1572872 | tf_op jit(solution)/shard_map/ppermute | solution.py:240
  218.2 22.2 %collective-permute-start.35 = (bf16[2,512,256]{2,1,0:T(8,128)(2,1)S(1)}, bf16[2,512,256]{2,1,0:T(8,128)(2,1)S(1)}, u32[]{:S(2)}, u32[]{:S(2)}) collective-permute-start(bf16[2,512,256]{2,1,0:T(8,128)(2,1)S(1)} %get-tuple-element.70), channel_id=1, source_target_pairs={{0,1},{1,0},{2,3},{3,2},{4,5},{5,4},{6,7},{7,6},{8,9},{9,8},{10,11... | collective-permute-start | bytes 1572872 | tf_op jit(solution)/shard_map/ppermute | solution.py:240
  229.4 13.0 %collective-permute-start.28 = (bf16[2,512,256]{2,1,0:T(8,128)(2,1)S(1)}, bf16[2,512,256]{2,1,0:T(8,128)(2,1)S(1)}, u32[]{:S(2)}, u32[]{:S(2)}) collective-permute-start(bf16[2,512,256]{2,1,0:T(8,128)(2,1)S(1)} %get-tuple-element.65), channel_id=1, source_target_pairs={{0,1},{1,0},{2,3},{3,2},{4,5},{5,4},{6,7},{7,6},{8,9},{9,8},{10,11... | collective-permute-start | bytes 1572872 | tf_op jit(solution)/shard_map/ppermute | solution.py:240
  240.4 2.5 collective-permute-start.21
  240.6 9.2 %collective-permute-start.36 = (bf16[1,512,256]{2,1,0:T(8,128)(2,1)S(1)}, bf16[1,512,256]{2,1,0:T(8,128)(2,1)S(1)}, u32[]{:S(2)}, u32[]{:S(2)}) collective-permute-start(bf16[1,512,256]{2,1,0:T(8,128)(2,1)S(1)} %fusion.5), channel_id=1, source_target_pairs={{0,2},{1,3},{2,0},{3,1},{4,6},{5,7},{6,4},{7,5},{8,10},{9,11},{10,... | collective-permute-start | bytes 786440 | tf_op jit(solution)/shard_map/ppermute | solution.py:240
  242.6 12.9 %collective-permute-start.29 = (bf16[1,512,256]{2,1,0:T(8,128)(2,1)S(1)}, bf16[1,512,256]{2,1,0:T(8,128)(2,1)S(1)}, u32[]{:S(2)}, u32[]{:S(2)}) collective-permute-start(bf16[1,512,256]{2,1,0:T(8,128)(2,1)S(1)} %fusion.4), channel_id=1, source_target_pairs={{0,2},{1,3},{2,0},{3,1},{4,6},{5,7},{6,4},{7,5},{8,10},{9,11},{10,... | collective-permute-start | bytes 786440 | tf_op jit(solution)/shard_map/ppermute | solution.py:240
  243.1 17.5 %collective-permute-start.22 = (bf16[1,512,256]{2,1,0:T(8,128)(2,1)S(1)}, bf16[1,512,256]{2,1,0:T(8,128)(2,1)S(1)}, u32[]{:S(2)}, u32[]{:S(2)}) collective-permute-start(bf16[1,512,256]{2,1,0:T(8,128)(2,1)S(1)} %fusion.3), channel_id=1, source_target_pairs={{0,2},{1,3},{2,0},{3,1},{4,6},{5,7},{6,4},{7,5},{8,10},{9,11},{10,... | collective-permute-start | bytes 786440 | tf_op jit(solution)/shard_map/ppermute | solution.py:240
  249.9 10.9 %collective-permute-start.37 = (bf16[4,64,256]{2,1,0:T(8,128)(2,1)S(1)}, bf16[4,64,256]{2,1,0:T(8,128)(2,1)S(1)}, u32[]{:S(2)}, u32[]{:S(2)}) collective-permute-start(bf16[4,64,256]{2,1,0:T(8,128)(2,1)S(1)} %fusion.11), channel_id=1, source_target_pairs={{0,4},{4,0},{8,12},{12,8},{16,20},{20,16},{24,28},{28,24},{1,5},{5... | collective-permute-start | bytes 393224 | tf_op jit(solution)/shard_map/ppermute | solution.py:367
  255.6 5.4 %collective-permute-start.30 = (bf16[4,64,256]{2,1,0:T(8,128)(2,1)S(1)}, bf16[4,64,256]{2,1,0:T(8,128)(2,1)S(1)}, u32[]{:S(2)}, u32[]{:S(2)}) collective-permute-start(bf16[4,64,256]{2,1,0:T(8,128)(2,1)S(1)} %fusion.10), channel_id=1, source_target_pairs={{0,4},{4,0},{8,12},{12,8},{16,20},{20,16},{24,28},{28,24},{1,5},{5... | collective-permute-start | bytes 393224 | tf_op jit(solution)/shard_map/ppermute | solution.py:367
  260.7 15.6 %copy-start.1 = (bf16[2,640,1280]{2,1,0:T(8,128)(2,1)S(1)}, bf16[2,640,1280]{2,1,0:T(8,128)(2,1)}, u32[]{:S(2)}) copy-start(bf16[2,640,1280]{2,1,0:T(8,128)(2,1)} %param.17) | copy-start | bytes 9830404
  260.7 5.1 %collective-permute-start.23 = (bf16[4,64,256]{2,1,0:T(8,128)(2,1)S(1)}, bf16[4,64,256]{2,1,0:T(8,128)(2,1)S(1)}, u32[]{:S(2)}, u32[]{:S(2)}) collective-permute-start(bf16[4,64,256]{2,1,0:T(8,128)(2,1)S(1)} %fusion.9), channel_id=1, source_target_pairs={{0,4},{4,0},{8,12},{12,8},{16,20},{20,16},{24,28},{28,24},{1,5},{5... | collective-permute-start | bytes 393224 | tf_op jit(solution)/shard_map/ppermute | solution.py:367
  260.9 5.1 %collective-permute-start.38 = (bf16[2,64,256]{2,1,0:T(8,128)(2,1)S(1)}, bf16[2,64,256]{2,1,0:T(8,128)(2,1)S(1)}, u32[]{:S(2)}, u32[]{:S(2)}) collective-permute-start(bf16[2,64,256]{2,1,0:T(8,128)(2,1)S(1)} %fusion.20), channel_id=1, source_target_pairs={{0,8},{4,12},{8,0},{12,4},{16,24},{20,28},{24,16},{28,20},{1,9},{5... | collective-permute-start | bytes 196616 | tf_op jit(solution)/shard_map/ppermute | solution.py:367
  261.0 6.2 %collective-permute-start.31 = (bf16[2,64,256]{2,1,0:T(8,128)(2,1)S(1)}, bf16[2,64,256]{2,1,0:T(8,128)(2,1)S(1)}, u32[]{:S(2)}, u32[]{:S(2)}) collective-permute-start(bf16[2,64,256]{2,1,0:T(8,128)(2,1)S(1)} %fusion.19), channel_id=1, source_target_pairs={{0,8},{4,12},{8,0},{12,4},{16,24},{20,28},{24,16},{28,20},{1,9},{5... | collective-permute-start | bytes 196616 | tf_op jit(solution)/shard_map/ppermute | solution.py:367
  265.9 4.4 %collective-permute-start.24 = (bf16[2,64,256]{2,1,0:T(8,128)(2,1)S(1)}, bf16[2,64,256]{2,1,0:T(8,128)(2,1)S(1)}, u32[]{:S(2)}, u32[]{:S(2)}) collective-permute-start(bf16[2,64,256]{2,1,0:T(8,128)(2,1)S(1)} %fusion.18), channel_id=1, source_target_pairs={{0,8},{4,12},{8,0},{12,4},{16,24},{20,28},{24,16},{28,20},{1,9},{5... | collective-permute-start | bytes 196616 | tf_op jit(solution)/shard_map/ppermute | solution.py:367
  266.0 4.9 %collective-permute-start.39 = (bf16[1,64,256]{2,1,0:T(8,128)(2,1)S(1)}, bf16[1,64,256]{2,1,0:T(8,128)(2,1)S(1)}, u32[]{:S(2)}, u32[]{:S(2)}) collective-permute-start(bf16[1,64,256]{2,1,0:T(8,128)(2,1)S(1)} %fusion.26), channel_id=1, source_target_pairs={{0,16},{4,20},{8,24},{12,28},{16,0},{20,4},{24,8},{28,12},{1,17},{... | collective-permute-start | bytes 98312 | tf_op jit(solution)/shard_map/ppermute | solution.py:367
  267.3 5.9 %collective-permute-start.32 = (bf16[1,64,256]{2,1,0:T(8,128)(2,1)S(1)}, bf16[1,64,256]{2,1,0:T(8,128)(2,1)S(1)}, u32[]{:S(2)}, u32[]{:S(2)}) collective-permute-start(bf16[1,64,256]{2,1,0:T(8,128)(2,1)S(1)} %fusion.25), channel_id=1, source_target_pairs={{0,16},{4,20},{8,24},{12,28},{16,0},{20,4},{24,8},{28,12},{1,17},{... | collective-permute-start | bytes 98312 | tf_op jit(solution)/shard_map/ppermute | solution.py:367
  270.3 5.2 %collective-permute-start.25 = (bf16[1,64,256]{2,1,0:T(8,128)(2,1)S(1)}, bf16[1,64,256]{2,1,0:T(8,128)(2,1)S(1)}, u32[]{:S(2)}, u32[]{:S(2)}) collective-permute-start(bf16[1,64,256]{2,1,0:T(8,128)(2,1)S(1)} %fusion.24), channel_id=1, source_target_pairs={{0,16},{4,20},{8,24},{12,28},{16,0},{20,4},{24,8},{28,12},{1,17},{... | collective-permute-start | bytes 98312 | tf_op jit(solution)/shard_map/ppermute | solution.py:367
where the time goes:
time: 277 us; the launch traced here: 276 us
  waiting for transfers between devices  98.2 us (35%)
  Pallas kernels  78.8 us (28%)
  starting transfers between devices  54.7 us (20%)
  local copies, waits for them, and re-layouts  29 us (10%)
  blocking collectives  7.85 us (3%)
  other arithmetic  6.82 us (2%)
    ppermute x18, waiting for transfers between devices, beside(): lax.ppermute(x, 'narrow', [(i, i ^ mask) for i in range(narrow_count)])  47 us
    pallas_call x4, Pallas kernels, density_call(): pl.pallas_call(functools.partial(density_kernel, count, groups), out_shap...  33.9 us
    pallas_call x2, Pallas kernels, block_call(): pl.pallas_call(functools.partial(block_kernel, count, groups, first), out...  26.9 us
    pallas_call x3, Pallas kernels, project_call(): pl.pallas_call(functools.partial(project_kernel, len(part_list)), out_sha...  18 us
    ppermute x7, starting transfers between devices, across(): return lax.ppermute(x, 'wide', pairs)  15.5 us
    ppermute x18, starting transfers between devices, beside(): lax.ppermute(x, 'narrow', [(i, i ^ mask) for i in range(narrow_count)])  14.9 us
    ppermute x3, waiting for transfers between devices, upward(): lax.ppermute(x, 'wide', [(i, i + 2) for i in range(wide_count - 2) if i /...  12.7 us
    unnamed x36, local copies, waits for them, and re-layouts  11.6 us
  transfers between devices with their start and end apart: 42, of which 22 were waited for; matrix products, arithmetic and copies ran while one was open for 8% of the time, Pallas kernels for 16%

commit v1 on v0

--- a/solution.py
+++ b/solution.py
@@ -13,58 +13,65 @@
 FIELDS = 3
 TOP = 2
 NBAT = 2
+UNROLL = 2
 ANY = pl.BlockSpec(memory_space=pl.ANY)
 VMEM = pl.BlockSpec(memory_space=pltpu.VMEM)
 SMEM = pl.BlockSpec(memory_space=pltpu.SMEM)
-
-
-def density_kernel(count, groups, slot_ref, dest_ref, row_ref, col_ref, *refs):
+VMEM_LIMIT = 60 * 1024 * 1024
+
+
+def density_kernel(count, order_ref, slot_ref, dest_ref, row_ref, col_ref, *refs):
     ao_refs = refs[:count]
-    tile_refs = refs[count : count + groups]
-    out_ref, held, sems = refs[count + groups :]
+    tile_ref, out_ref, held, total, sems = refs[count:]
     copies = [pltpu.make_async_copy(ao_refs[i], held.at[i], sems.at[i]) for i in range(count)]
     for copy in copies:
         copy.start()
-    out_ref[...] = jnp.zeros_like(out_ref)
+    total[...] = jnp.zeros_like(total)
     for copy in copies:
         copy.wait()
-    tiles = tile_refs[0].shape[0]
     points = held.shape[2]
-    for group in range(groups):
-        tile_ref = tile_refs[group]
-
-        def step(i, carry, group=group, tile_ref=tile_ref):
-            at = group * tiles * TOP + i
-            slot = slot_ref[at]
-
-            @pl.when(slot >= 0)
-            def _():
-                left = tile_ref[i // TOP]
-                rows = pl.ds(pl.multiple_of(row_ref[at] * BLK, BLK), BLK)
-                cols = pl.ds(pl.multiple_of(col_ref[at] * BLK, BLK), BLK)
-                dest = dest_ref[at]
-                for low in range(0, points, 256):
-                    lanes = slice(low, min(low + 256, points))
-                    mixed = jnp.dot(left, held[slot, cols, lanes], preferred_element_type=jnp.float32)
-                    mixed = mixed.reshape(FIELDS, BLK, mixed.shape[-1])
-                    value = held[slot, rows, lanes].astype(jnp.float32)
-                    out_ref[dest, :, lanes] += jnp.sum(mixed * value[None], axis=1)
-
-            return carry
-
-        lax.fori_loop(0, tiles * TOP, step, 0)
-
-
-def density_call(slots, dests, rows, cols, ao_list, tile_list, wide_count):
-    count, groups = len(ao_list), len(tile_list)
+    last = tile_ref.shape[0] - 1
+
+    def one(at):
+        slot = slot_ref[at]
+        left = tile_ref[jnp.minimum(at // TOP, last)]
+        rows = pl.ds(pl.multiple_of(row_ref[at] * BLK, BLK), BLK)
+        cols = pl.ds(pl.multiple_of(col_ref[at] * BLK, BLK), BLK)
+        sums = []
+        for low in range(0, points, 256):
+            lanes = slice(low, min(low + 256, points))
+            mixed = jnp.dot(left, held[slot, cols, lanes], preferred_element_type=jnp.float32)
+            width = mixed.shape[-1]
+            value = held[slot, rows, lanes].astype(jnp.float32)
+            product = mixed.reshape(FIELDS, BLK, width) * value[None]
+            sums.append((lanes, jnp.sum(product.reshape(FIELDS, BLK // 8, 8, width), axis=1)))
+        return sums
+
+    def step(i, carry):
+        found = [order_ref[UNROLL * i + u] for u in range(UNROLL)]
+        values = [one(at) for at in found]
+        for at, sums in zip(found, values):
+            dest = dest_ref[at]
+            for lanes, value in sums:
+                total[dest, :, :, lanes] += value
+        return carry
+
+    steps = (order_ref[order_ref.shape[0] - 1] + UNROLL - 1) // UNROLL
+    lax.fori_loop(0, steps, step, 0)
+    out_ref[...] = jnp.sum(total[: out_ref.shape[0]], axis=2)
+
+
+def density_call(order, slots, dests, rows, cols, ao_list, tiles, wide_count):
+    count = len(ao_list)
     height, points = ao_list[0].shape
     return pl.pallas_call(
-        functools.partial(density_kernel, count, groups),
+        functools.partial(density_kernel, count),
         out_shape=jax.ShapeDtypeStruct((wide_count, FIELDS, points), jnp.float32),
-        in_specs=[SMEM] * 4 + [ANY] * count + [VMEM] * groups,
+        in_specs=[SMEM] * 5 + [ANY] * count + [VMEM],
         out_specs=VMEM,
         scratch_shapes=[
             pltpu.VMEM((count, height, points), jnp.bfloat16),
+            pltpu.VMEM((wide_count + 1, FIELDS, 8, points), jnp.float32),
             pltpu.SemaphoreType.DMA((count,)),
         ],
         compiler_params=pltpu.CompilerParams(vmem_limit_bytes=24 * 1024 * 1024),
@@ -72,7 +79,7 @@
             flops=1_000_000_000, bytes_accessed=10_000_000, transcendentals=0
         ),
         name="density",
-    )(slots, dests, rows, cols, *ao_list, *tile_list)
+    )(order, slots, dests, rows, cols, *ao_list, tiles)
 
 
 def block_kernel(count, groups, first, place_ref, slot_ref, row_ref, col_ref, pot_ref, *refs):
@@ -134,7 +141,7 @@
             pltpu.VMEM((FIELDS, BLK, BLK), jnp.float32),
             pltpu.SemaphoreType.DMA((count,)),
         ],
-        compiler_params=pltpu.CompilerParams(vmem_limit_bytes=40 * 1024 * 1024),
+        compiler_params=pltpu.CompilerParams(vmem_limit_bytes=VMEM_LIMIT),
         cost_estimate=pl.CostEstimate(
             flops=2_000_000_000 * groups, bytes_accessed=10_000_000, transcendentals=0
         ),
@@ -288,14 +295,40 @@
     other = (dests ^ wide) & 1
     occ_sel = occ_coef.reshape(-1, BLK, nocc)[tile_rows].transpose(0, 2, 1)
     vir_sel = vir_coef.reshape(-1, BLK, nvir)[tile_cols].reshape(tile_count * BLK, nvir)
-    dests, occ_sel, vir_sel = lax.optimization_barrier((dests, occ_sel, vir_sel))
+    stages = jnp.arange(line)[:, None]
+    active = mine[None] & (jnp.abs(offset)[None] == stages)
+    indices = jnp.where(stages > 0, other[None] + 2 * (offset > 0).astype(jnp.int32)[None], other)
+    count = dests.shape[0]
+    spots = jnp.arange(count)
+    earlier = spots[None, :] < spots[:, None]
+    rank = jnp.sum((active[:, None, :] & earlier[None]).astype(jnp.int32), axis=2)
+    hit = active[:, None, :] & (rank[:, None, :] == spots[None, :, None])
+    order = jnp.sum(jnp.where(hit, spots - count, 0), axis=2) + count
+    sizes = jnp.sum(active.astype(jnp.int32), axis=1)
+    fill = jnp.full((line, UNROLL), count, jnp.int32)
+    order = jnp.concatenate([order, fill, sizes[:, None]], axis=1)
+
+    def extend(x, value):
+        return jnp.concatenate([x, jnp.full((1,), value, jnp.int32)])
+
+    more_dests, more_rows, more_cols = extend(dests, wide_count), extend(rows, 0), extend(cols, 0)
+    all_tiles = jnp.concatenate(tile_list, axis=0)
+    order, occ_sel, vir_sel = lax.optimization_barrier((order, occ_sel, vir_sel))
     density = None
     for k in range(line):
-        index = other + 2 * (offset > 0).astype(jnp.int32) if k else other
-        slots = jnp.where(mine & (jnp.abs(offset) == k), index, -1)
+        stage_order = order[k]
         if density is not None:
-            slots, density = lax.optimization_barrier((slots, density))
-        part = density_call(slots, dests, rows, cols, ao_stages[k], tile_list, wide_count)
+            stage_order, density = lax.optimization_barrier((stage_order, density))
+        part = density_call(
+            stage_order,
+            extend(indices[k], 0),
+            more_dests,
+            more_rows,
+            more_cols,
+            ao_stages[k],
+            all_tiles,
+            wide_count,
+        )
         density = part if density is None else density + part
     density = lax.all_to_all(density, "wide", split_axis=0, concat_axis=0, tiled=True)
     density = jnp.sum(density, axis=0)
@@ -354,7 +387,8 @@
         even, odd = project_call(where, [near_sum[f], far_sum[f]], occ_sel, vir_sel, narrow_count)
         mask = 1
         while True:
-            even = even + beside(odd, mask).astype(jnp.float32)
+            received = beside(odd, mask)
+            even = even + received.astype(jnp.float32)
             mask *= 2
             if mask == narrow_count:
                 break

time: 277 us -> 285 us (1.029)
  waiting for transfers between devices: 98.2 us -> 110 us
  Pallas kernels: 78.8 us -> 68.1 us
  starting transfers between devices: 54.7 us -> 62.8 us
  blocking collectives: 7.85 us -> 0 us
  other arithmetic: 6.82 us -> 12.7 us
    ppermute x18, waiting for transfers between devices: 47 us -> 63.7 us  [beside(): lax.ppermute(x, 'narrow', [(i, i ^ mask) for i in range(narrow_count)])]
    pallas_call x4, Pallas kernels: 33.9 us -> 19.1 us  [density_call(): pl.pallas_call(functools.partial(density_kernel, count), out_shape=jax.Sh...]
    ppermute x3, waiting for transfers between devices: 12.7 us -> 0.01 us  [upward(): lax.ppermute(x, 'wide', [(i, i + 2) for i in range(wide_count - 2) if i /...]
    all_to_all x1 -> x0, blocking collectives: 7.85 us -> none  [body(): lax.all_to_all(jnp.broadcast_to(routes, (narrow_count, routes.shape[1])),...]
    ppermute x3, waiting for transfers between devices: 8.67 us -> 14.9 us  [downward(): lax.ppermute(x, 'wide', [(i, i - 2) for i in range(2, wide_count) if i //...]
    all_to_all x1, starting transfers between devices: 3.97 us -> 9.02 us  [body(): lax.all_to_all(density, 'wide', split_axis=0, concat_axis=0, tiled=True)]
    convert_element_type x6, other arithmetic: 0.87 us -> 5.82 us  [fold(): (p.astype(jnp.float32) + beside(q, mask).astype(jnp.float32)).astype(jnp....]
    pallas_call x2, Pallas kernels: 26.9 us -> 31 us  [block_call(): pl.pallas_call(functools.partial(block_kernel, count, groups, first), out...]
  transfers between devices with their start and end apart: 42 -> 43, of which waited for: 22 -> 17; matrix products, arithmetic and copies ran while one was open for 8% -> 11% of each run, Pallas kernels for 16% -> 12%
where the time goes in v1:
time: 285 us; the launch traced here: 283 us
  waiting for transfers between devices  110 us (39%)
  Pallas kernels  68.1 us (24%)
  starting transfers between devices  62.8 us (22%)
  local copies, waits for them, and re-layouts  28.6 us (10%)
  other arithmetic  12.7 us (4%)
    ppermute x18, waiting for transfers between devices, beside(): lax.ppermute(x, 'narrow', [(i, i ^ mask) for i in range(narrow_count)])  63.7 us
    pallas_call x2, Pallas kernels, block_call(): pl.pallas_call(functools.partial(block_kernel, count, groups, first), out...  31 us
    pallas_call x4, Pallas kernels, density_call(): pl.pallas_call(functools.partial(density_kernel, count), out_shape=jax.Sh...  19.1 us
    pallas_call x3, Pallas kernels, project_call(): pl.pallas_call(functools.partial(project_kernel, len(part_list)), out_sha...  18 us
    ppermute x18, starting transfers between devices, beside(): lax.ppermute(x, 'narrow', [(i, i ^ mask) for i in range(narrow_count)])  16.9 us
    ppermute x3, waiting for transfers between devices, downward(): lax.ppermute(x, 'wide', [(i, i - 2) for i in range(2, wide_count) if i //...  14.9 us
    ppermute x7, starting transfers between devices, across(): return lax.ppermute(x, 'wide', pairs)  14.3 us
    ppermute x7, waiting for transfers between devices, across(): return lax.ppermute(x, 'wide', pairs)  12.5 us
  transfers between devices with their start and end apart: 43, of which 17 were waited for; matrix products, arithmetic and copies ran while one was open for 11% of the time, Pallas kernels for 12%

profile of v1, /device:TPU:0, one launch (start us, length us, event | category | flops | bytes accessed | tf_op | source)
XLA Modules:
  0.0 283.3 jit_solution(8170152860504921087)
XLA Ops:
  0.0 1.9 copy-done
  1.9 1.0 dynamic-slice_bitcast_fusion.refs_0_
  2.9 3.0 %collective-permute-start = (bf16[640,640]{1,0:T(8,128)(2,1)}, bf16[640,640]{1,0:T(8,128)(2,1)}, u32[]{:S(2)}, u32[]{:S(2)}) collective-permute-start(bf16[640,640]{1,0:T(8,128)(2,1)} %dynamic-slice_bitcast_fusion.refs_0_), channel_id=1, source_target_pairs={{0,4},{4,0},{8,12},{12,8},{16,20},{20,16},{24,28},{28,24},{1,5},{5... | collective-permute-start | bytes 2457608 | tf_op jit(solution)/shard_map/ppermute | solution.py:234
  5.9 3.5 %collective-permute-start.4 = (bf16[640,640]{1,0:T(8,128)(2,1)}, bf16[640,640]{1,0:T(8,128)(2,1)S(1)}, u32[]{:S(2)}, u32[]{:S(2)}) collective-permute-start(bf16[640,640]{1,0:T(8,128)(2,1)} %dynamic-slice_bitcast_fusion.refs_0_), channel_id=1, source_target_pairs={{0,8},{4,12},{8,16},{12,20},{16,24},{20,28},{1,9},{5,13},{9,17},{1... | collective-permute-start | bytes 2457608 | tf_op jit(solution)/shard_map/ppermute | solution.py:237
  9.4 1.3 collective-permute-start.6
  12.2 3.2 %all-to-all-start = ((s32[4,1,64]{2,1,0:T(1,128)}), s32[4,1,64]{2,1,0:T(1,128)S(1)}, u32[]{:S(2)}, u32[]{:S(2)}) async-start(s32[4,1,64]{2,1,0:T(1,128)} %broadcast_in_dim.82), calls=%async_computation | async-start | bytes 4096 | tf_op jit(solution)/shard_map/all_to_all | solution.py:271
  16.9 3.6 %gather_fusion.1 = bf16[16,128,512]{2,1,0:T(8,128)(2,1)} fusion(bf16[16,128,512]{2,1,0:T(8,128)(2,1)} %bitcast.160, s32[1024]{0:T(1024)S(1)} %get-tuple-element.97), kind=kCustom, calls=%fused_computation.1 | custom fusion | bytes 4194368 | tf_op jit(solution)/shard_map/gather | solution.py:296
  20.5 3.0 %copy.52 = bf16[16,128,512]{1,2,0:T(8,128)(2,1)S(1)} copy(bf16[16,128,512]{2,1,0:T(8,128)(2,1)} %gather_fusion.1) | data formatting | bytes 4194304 | tf_op jit(solution)/shard_map/gather | solution.py:296
  23.5 6.2 %gather_fusion.2 = bf16[16,128,1024]{2,1,0:T(8,128)(2,1)} fusion(bf16[32,128,1024]{2,1,0:T(8,128)(2,1)} %bitcast.159, s32[1024]{0:T(1024)S(1)} %get-tuple-element.96), kind=kCustom, calls=%fused_computation.2 | custom fusion | bytes 8388672 | tf_op jit(solution)/shard_map/gather | solution.py:297
  30.2 1.6 collective-permute-start.2
  33.9 1.6 collective-permute-start.8
  35.5 1.3 collective-permute-start.10
  37.0 30.1 %collective-permute-done.2 = bf16[16,384,128]{2,1,0:T(8,128)(2,1)} collective-permute-done((bf16[16,384,128]{2,1,0:T(8,128)(2,1)}, bf16[16,384,128]{2,1,0:T(8,128)(2,1)}, u32[]{:S(2)}, u32[]{:S(2)}) %collective-permute-start.2) | collective-permute-done | bytes 1572896 | tf_op jit(solution)/shard_map/ppermute | solution.py:247
  67.2 0.7 collective-permute-start.5
  67.9 0.7 collective-permute-start.12
  68.7 1.3 collective-permute-start.14
  70.0 1.6 constant_dynamic-update-slice_fusion.3
  71.6 2.4 collective-permute-start.7
  74.1 0.7 collective-permute-start.9
  74.8 3.4 %collective-permute-start.11 = (bf16[640,640]{1,0:T(8,128)(2,1)}, bf16[640,640]{1,0:T(8,128)(2,1)S(1)}, u32[]{:S(2)}, u32[]{:S(2)}) collective-permute-start(bf16[640,640]{1,0:T(8,128)(2,1)} %collective-permute-done.10.refs_2_.refs_8_), channel_id=1, source_target_pairs={{0,4},{4,0},{8,12},{12,8},{1,5},{5,1},{9,13},{13,9},{2,6},{6,2},{1... | collective-permute-start | bytes 2457608 | tf_op jit(solution)/shard_map/ppermute | solution.py:234
  78.2 14.9 %collective-permute-done.14.refs_2_.refs_12_ = bf16[640,640]{1,0:T(8,128)(2,1)S(1)} collective-permute-done((bf16[640,640]{1,0:T(8,128)(2,1)}, bf16[640,640]{1,0:T(8,128)(2,1)S(1)}, u32[]{:S(2)}, u32[]{:S(2)}) %collective-permute-start.14) | collective-permute-done | bytes 819232 | tf_op jit(solution)/shard_map/ppermute | solution.py:242
  93.9 3.4 %collective-permute-start.15 = (bf16[640,640]{1,0:T(8,128)(2,1)S(1)}, bf16[640,640]{1,0:T(8,128)(2,1)S(1)}, u32[]{:S(2)}, u32[]{:S(2)}) collective-permute-start(bf16[640,640]{1,0:T(8,128)(2,1)S(1)} %collective-permute-done.14.refs_2_.refs_12_), channel_id=1, source_target_pairs={{0,4},{4,0},{1,5},{5,1},{2,6},{6,2},{3,7},{7,3}} | collective-permute-start | bytes 2457608 | tf_op jit(solution)/shard_map/ppermute | solution.py:234
  97.3 1.7 constant_dynamic-update-slice_fusion.2
  99.0 1.7 constant_dynamic-update-slice_fusion.1
  100.9 5.4 %density.4 = f32[8,3,640]{2,1,0:T(4,128)S(1)} custom-call(s32[131]{0:T(256)S(1)} %bitcast.158, s32[129]{0:T(256)S(1)} %pad_add_fusion.6.slot_ref, s32[129]{0:T(256)S(1)} %pad_add_fusion.8.dest_ref, s32[129]{0:T(256)S(1)} %get-tuple-element.100.row_ref, s32[129]{0:T(256)S(1)} %get-tuple-element.99.col_ref, ...), custom_call_target="tpu_custom_call" | custom-call | flops 1000000000 | bytes 10000000 | tf_op jit(solution)/shard_map/density/pallas_call | solution.py:67
  106.3 4.6 %density.5 = f32[8,3,640]{2,1,0:T(4,128)S(1)} custom-call(s32[131]{0:T(256)S(1)} %bitcast.157, s32[129]{0:T(256)S(1)} %pad_add_fusion.3.slot_ref, s32[129]{0:T(256)S(1)} %pad_add_fusion.8.dest_ref, s32[129]{0:T(256)S(1)} %get-tuple-element.100.row_ref, s32[129]{0:T(256)S(1)} %get-tuple-element.99.col_ref, ...), custom_call_target="tpu_custom_call" | custom-call | flops 1000000000 | bytes 10000000 | tf_op jit(solution)/shard_map/density/pallas_call | solution.py:67
  111.0 1.4 collective-permute-done.11.refs_3_.refs_9_
  112.4 5.9 %density.6 = f32[8,3,640]{2,1,0:T(4,128)S(1)} custom-call(s32[131]{0:T(256)S(1)} %bitcast.156, s32[129]{0:T(256)S(1)} %pad_add_fusion.2.slot_ref, s32[129]{0:T(256)S(1)} %pad_add_fusion.8.dest_ref, s32[129]{0:T(256)S(1)} %get-tuple-element.100.row_ref, s32[129]{0:T(256)S(1)} %get-tuple-element.99.col_ref, ...), custom_call_target="tpu_custom_call" | custom-call | flops 1000000000 | bytes 10000000 | tf_op jit(solution)/shard_map/density/pallas_call | solution.py:67
  118.3 11.1 %collective-permute-done.15.refs_3_.refs_13_ = bf16[640,640]{1,0:T(8,128)(2,1)S(1)} collective-permute-done((bf16[640,640]{1,0:T(8,128)(2,1)S(1)}, bf16[640,640]{1,0:T(8,128)(2,1)S(1)}, u32[]{:S(2)}, u32[]{:S(2)}) %collective-permute-start.15) | collective-permute-done | bytes 819232 | tf_op jit(solution)/shard_map/ppermute | solution.py:234
  129.5 3.3 %density.7 = f32[8,3,640]{2,1,0:T(4,128)S(1)} custom-call(s32[131]{0:T(256)S(1)} %bitcast.155, s32[129]{0:T(256)S(1)} %pad_add_fusion.1.slot_ref, s32[129]{0:T(256)S(1)} %pad_add_fusion.8.dest_ref, s32[129]{0:T(256)S(1)} %get-tuple-element.100.row_ref, s32[129]{0:T(256)S(1)} %get-tuple-element.99.col_ref, ...), custom_call_target="tpu_custom_call" | custom-call | flops 1000000000 | bytes 10000000 | tf_op jit(solution)/shard_map/density/pallas_call | solution.py:67
  133.4 9.0 %all-to-all-start.1 = ((f32[8,3,640]{2,1,0:T(4,128)}), f32[8,3,640]{2,1,0:T(4,128)S(1)}, u32[]{:S(2)}, u32[]{:S(2)}) async-start(f32[8,3,640]{2,1,0:T(4,128)} %add.215), calls=%async_computation.1 | async-start | bytes 163840 | tf_op jit(solution)/shard_map/all_to_all | solution.py:333
  143.1 0.8 dynamic-slice_reduce_fusion.1
  143.9 1.4 fusion.30
  145.3 4.1 %all-to-all-done.1 = f32[8,3,640]{2,1,0:T(4,128)S(1)} async-done(((f32[8,3,640]{2,1,0:T(4,128)}), f32[8,3,640]{2,1,0:T(4,128)S(1)}, u32[]{:S(2)}, u32[]{:S(2)}) %all-to-all-start.1) | async-done | bytes 61472 | tf_op jit(solution)/shard_map/all_to_all | solution.py:333
  150.1 3.5 %all-to-all-start.2 = ((f32[8,3,640]{2,1,0:T(4,128)}), f32[8,3,640]{2,1,0:T(4,128)S(1)}, u32[]{:S(2)}, u32[]{:S(2)}) async-start(f32[8,3,640]{2,1,0:T(4,128)} %broadcast_in_dim.93), calls=%async_computation.2 | async-start | bytes 163840 | tf_op jit(solution)/shard_map/all_to_all | solution.py:345
  154.4 6.0 %all-to-all-done.2.pot_ref = f32[8,3,640]{2,1,0:T(4,128)S(1)} async-done(((f32[8,3,640]{2,1,0:T(4,128)}), f32[8,3,640]{2,1,0:T(4,128)S(1)}, u32[]{:S(2)}, u32[]{:S(2)}) %all-to-all-start.2) | async-done | bytes 61472 | tf_op jit(solution)/shard_map/all_to_all | solution.py:345
  161.1 13.9 %blocks.2 = (bf16[16,128,128]{2,1,0:T(8,128)(2,1)}, bf16[16,128,128]{2,1,0:T(8,128)(2,1)}, bf16[16,128,128]{2,1,0:T(8,128)(2,1)}, bf16[16,128,128]{2,1,0:T(8,128...) custom-call(s32[14]{0:T(128)} %stack.82.place_ref, s32[128]{0:T(128)} %get-tuple-element.93.slot_ref, ...), custom_call_target="tpu_custom_call" | custom-call | flops 4000000000 | bytes 10000000 | tf_op jit(solution)/shard_map/blocks/pallas_call | solution.py:134
  175.6 1.5 collective-permute-done.16
  177.1 1.2 add_convert_fusion.5
  178.3 2.0 add_convert_fusion.4
  180.3 1.2 add_convert_fusion.3
  181.5 17.1 %blocks.3 = (bf16[16,128,128]{2,1,0:T(8,128)(2,1)}, bf16[16,128,128]{2,1,0:T(8,128)(2,1)}, bf16[16,128,128]{2,1,0:T(8,128)(2,1)}, bf16[16,128,128]{2,1,0:T(8,128...) custom-call(s32[14]{0:T(128)} %stack.82.place_ref, s32[128]{0:T(128)} %get-tuple-element.93.slot_ref, ...), custom_call_target="tpu_custom_call" | custom-call | flops 4000000000 | bytes 10000000 | tf_op jit(solution)/shard_map/blocks/pallas_call | solution.py:134
  198.9 7.5 %collective-permute-start.34 = (bf16[16,128,128]{2,1,0:T(8,128)(2,1)S(1)}, bf16[16,128,128]{2,1,0:T(8,128)(2,1)S(1)}, u32[]{:S(2)}, u32[]{:S(2)}) collective-permute-start(bf16[16,128,128]{2,1,0:T(8,128)(2,1)S(1)} %add_convert_fusion.3), channel_id=1, source_target_pairs={{0,2},{1,3},{2,0},{3,1},{4,6},{5,7},{6,4},{7,5},{8,10},{9,11},{10,... | collective-permute-start | bytes 1572872 | tf_op jit(solution)/shard_map/ppermute | solution.py:247
  207.0 1.7 collective-permute-start.20
  208.7 1.2 add_convert_fusion.refs_0_
  209.9 9.2 %collective-permute-done.34.refs_1_ = bf16[16,128,128]{2,1,0:T(8,128)(2,1)S(1)} collective-permute-done((bf16[16,128,128]{2,1,0:T(8,128)(2,1)S(1)}, bf16[16,128,128]{2,1,0:T(8,128)(2,1)S(1)}, u32[]{:S(2)}, u32[]{:S(2)}) %collective-permute-start.34) | collective-permute-done | bytes 524320 | tf_op jit(solution)/shard_map/ppermute | solution.py:247
  219.1 2.2 copy-done.2
  221.3 6.0 %project.5 = (f32[2,512,256]{2,1,0:T(8,128)S(1)}, bf16[2,512,256]{2,1,0:T(8,128)(2,1)S(1)}) custom-call(s32[10]{0:T(128)S(1)} %pad_add_fusion.9.where_ref, bf16[16,128,128]{2,1,0:T(8,128)(2,1)S(1)} %add_convert_fusion.refs_0_, bf16[16,128,128]{2,1,0:T(8,128)(2,1)S(1)} %collective-permute-done.34.refs_1_, bf16[16,512,128]{2,1,0:T(8,128)(2,1)S(1)} %bitcast.152, ...), custom_call_target="tpu_custom_call" | custom-call | flops 2400000000 | bytes 10000000 | tf_op jit(solution)/shard_map/project/pallas_call | solution.py:189
  227.6 2.8 collective-permute-done.27.refs_1_
  230.4 6.0 %project.4 = (f32[2,512,256]{2,1,0:T(8,128)S(1)}, bf16[2,512,256]{2,1,0:T(8,128)(2,1)S(1)}) custom-call(s32[10]{0:T(128)S(1)} %pad_add_fusion.9.where_ref, bf16[16,128,128]{2,1,0:T(8,128)(2,1)S(1)} %add_convert_fusion.1.refs_0_, bf16[16,128,128]{2,1,0:T(8,128)(2,1)S(1)} %collective-permute-done.27.refs_1_, bf16[16,512,128]{2,1,0:T(8,128)(2,1)S(1)} %bitcast.153, ...), custom_call_target="tpu_custom_call" | custom-call | flops 2400000000 | bytes 10000000 | tf_op jit(solution)/shard_map/project/pallas_call | solution.py:189
  236.6 4.7 %collective-permute-done.20.refs_1_ = bf16[16,128,128]{2,1,0:T(8,128)(2,1)S(1)} collective-permute-done((bf16[16,128,128]{2,1,0:T(8,128)(2,1)S(1)}, bf16[16,128,128]{2,1,0:T(8,128)(2,1)S(1)}, u32[]{:S(2)}, u32[]{:S(2)}) %collective-permute-start.20) | collective-permute-done | bytes 524320 | tf_op jit(solution)/shard_map/ppermute | solution.py:247
  241.3 6.0 %project.3 = (f32[2,512,256]{2,1,0:T(8,128)S(1)}, bf16[2,512,256]{2,1,0:T(8,128)(2,1)S(1)}) custom-call(s32[10]{0:T(128)S(1)} %pad_add_fusion.9.where_ref, bf16[16,128,128]{2,1,0:T(8,128)(2,1)S(1)} %add_convert_fusion.2.refs_0_, bf16[16,128,128]{2,1,0:T(8,128)(2,1)S(1)} %collective-permute-done.20.refs_1_, bf16[16,512,128]{2,1,0:T(8,128)(2,1)S(1)} %bitcast.154, ...), custom_call_target="tpu_custom_call" | custom-call | flops 2400000000 | bytes 10000000 | tf_op jit(solution)/shard_map/project/pallas_call | solution.py:189
  247.6 1.8 collective-permute-start.36
  250.0 1.8 collective-permute-start.22
  251.8 5.0 %collective-permute-done.36 = bf16[1,512,256]{2,1,0:T(8,128)(2,1)S(1)} collective-permute-done((bf16[1,512,256]{2,1,0:T(8,128)(2,1)S(1)}, bf16[1,512,256]{2,1,0:T(8,128)(2,1)S(1)}, u32[]{:S(2)}, u32[]{:S(2)}) %collective-permute-start.36) | collective-permute-done | bytes 262176 | tf_op jit(solution)/shard_map/ppermute | solution.py:247
  257.0 5.5 %collective-permute-done.29 = bf16[1,512,256]{2,1,0:T(8,128)(2,1)S(1)} collective-permute-done((bf16[1,512,256]{2,1,0:T(8,128)(2,1)S(1)}, bf16[1,512,256]{2,1,0:T(8,128)(2,1)S(1)}, u32[]{:S(2)}, u32[]{:S(2)}) %collective-permute-start.29) | collective-permute-done | bytes 262176 | tf_op jit(solution)/shard_map/ppermute | solution.py:247
  262.6 5.0 %collective-permute-done.22 = bf16[1,512,256]{2,1,0:T(8,128)(2,1)S(1)} collective-permute-done((bf16[1,512,256]{2,1,0:T(8,128)(2,1)S(1)}, bf16[1,512,256]{2,1,0:T(8,128)(2,1)S(1)}, u32[]{:S(2)}, u32[]{:S(2)}) %collective-permute-start.22) | collective-permute-done | bytes 262176 | tf_op jit(solution)/shard_map/ppermute | solution.py:247
  267.9 2.1 collective-permute-start.31
  270.0 2.8 collective-permute-done.23
  272.9 1.3 collective-permute-start.39
  274.2 1.8 collective-permute-start.32
  276.0 1.3 collective-permute-done.24
  278.0 2.1 collective-permute-done.32
  280.2 2.4 collective-permute-done.25
  (166 shorter events, 15.0 us)
Async XLA Ops:
  0.0 1.9 copy-start
  2.9 64.2 %collective-permute-start = (bf16[640,640]{1,0:T(8,128)(2,1)}, bf16[640,640]{1,0:T(8,128)(2,1)}, u32[]{:S(2)}, u32[]{:S(2)}) collective-permute-start(bf16[640,640]{1,0:T(8,128)(2,1)} %dynamic-slice_bitcast_fusion.refs_0_), channel_id=1, source_target_pairs={{0,4},{4,0},{8,12},{12,8},{16,20},{20,16},{24,28},{28,24},{1,5},{5... | collective-permute-start | bytes 2457608 | tf_op jit(solution)/shard_map/ppermute | solution.py:234
  5.9 28.0 %collective-permute-start.4 = (bf16[640,640]{1,0:T(8,128)(2,1)}, bf16[640,640]{1,0:T(8,128)(2,1)S(1)}, u32[]{:S(2)}, u32[]{:S(2)}) collective-permute-start(bf16[640,640]{1,0:T(8,128)(2,1)} %dynamic-slice_bitcast_fusion.refs_0_), channel_id=1, source_target_pairs={{0,8},{4,12},{8,16},{12,20},{16,24},{20,28},{1,9},{5,13},{9,17},{1... | collective-permute-start | bytes 2457608 | tf_op jit(solution)/shard_map/ppermute | solution.py:237
  9.4 26.1 %collective-permute-start.6 = (bf16[640,640]{1,0:T(8,128)(2,1)}, bf16[640,640]{1,0:T(8,128)(2,1)}, u32[]{:S(2)}, u32[]{:S(2)}) collective-permute-start(bf16[640,640]{1,0:T(8,128)(2,1)} %dynamic-slice_bitcast_fusion.refs_0_), channel_id=1, source_target_pairs={{8,0},{12,4},{16,8},{20,12},{24,16},{28,20},{9,1},{13,5},{17,9},{2... | collective-permute-start | bytes 2457608 | tf_op jit(solution)/shard_map/ppermute | solution.py:242
  12.2 17.5 %all-to-all-start = ((s32[4,1,64]{2,1,0:T(1,128)}), s32[4,1,64]{2,1,0:T(1,128)S(1)}, u32[]{:S(2)}, u32[]{:S(2)}) async-start(s32[4,1,64]{2,1,0:T(1,128)} %broadcast_in_dim.82), calls=%async_computation | async-start | bytes 4096 | tf_op jit(solution)/shard_map/all_to_all | solution.py:271
  29.7 41.8 %collective-permute-start.1 = (bf16[16,384,128]{2,1,0:T(8,128)(2,1)}, bf16[16,384,128]{2,1,0:T(8,128)(2,1)}, u32[]{:S(2)}, u32[]{:S(2)}) collective-permute-start(bf16[16,384,128]{2,1,0:T(8,128)(2,1)} %bitcast.167), channel_id=1, source_target_pairs={{0,1},{1,0},{2,3},{3,2},{4,5},{5,4},{6,7},{7,6},{8,9},{9,8},{10,11... | collective-permute-start | bytes 4718600 | tf_op jit(solution)/shard_map/ppermute | solution.py:247
  30.2 36.9 %collective-permute-start.2 = (bf16[16,384,128]{2,1,0:T(8,128)(2,1)}, bf16[16,384,128]{2,1,0:T(8,128)(2,1)}, u32[]{:S(2)}, u32[]{:S(2)}) collective-permute-start(bf16[16,384,128]{2,1,0:T(8,128)(2,1)} %bitcast.168), channel_id=1, source_target_pairs={{0,2},{1,3},{2,0},{3,1},{4,6},{5,7},{6,4},{7,5},{8,10},{9,11},{10,... | collective-permute-start | bytes 4718600 | tf_op jit(solution)/shard_map/ppermute | solution.py:247
  33.5 67.1 %copy-start.16 = (s32[128]{0:T(128)}, s32[128]{0:T(128)S(1)}, u32[]{:S(2)}) copy-start(s32[128]{0:T(128)S(1)} %get-tuple-element.95.row_ref) | copy-start | bytes 1540
  33.9 72.4 %copy-start.4 = (bf16[640,640]{1,0:T(8,128)(2,1)}, bf16[640,640]{1,0:T(8,128)(2,1)S(1)}, u32[]{:S(2)}) copy-start(bf16[640,640]{1,0:T(8,128)(2,1)S(1)} %collective-permute-done.4.refs_0_.refs_2_) | copy-start | bytes 2457604
  33.9 34.0 %collective-permute-start.8 = (bf16[640,640]{1,0:T(8,128)(2,1)S(1)}, bf16[640,640]{1,0:T(8,128)(2,1)}, u32[]{:S(2)}, u32[]{:S(2)}) collective-permute-start(bf16[640,640]{1,0:T(8,128)(2,1)S(1)} %collective-permute-done.4.refs_0_.refs_2_), channel_id=1, source_target_pairs={{8,16},{12,20},{16,24},{20,28},{9,17},{13,21},{17,25},{21,29},{10,... | collective-permute-start | bytes 2457608 | tf_op jit(solution)/shard_map/ppermute | solution.py:237
  35.5 33.1 %collective-permute-start.10 = (bf16[640,640]{1,0:T(8,128)(2,1)}, bf16[640,640]{1,0:T(8,128)(2,1)}, u32[]{:S(2)}, u32[]{:S(2)}) collective-permute-start(bf16[640,640]{1,0:T(8,128)(2,1)} %collective-permute-done.6.refs_2_.refs_4_), channel_id=1, source_target_pairs={{8,0},{12,4},{16,8},{20,12},{9,1},{13,5},{17,9},{21,13},{10,2},{14... | collective-permute-start | bytes 2457608 | tf_op jit(solution)/shard_map/ppermute | solution.py:242
  67.1 26.8 %collective-permute-start.3 = (bf16[16,384,128]{2,1,0:T(8,128)(2,1)}, bf16[16,384,128]{2,1,0:T(8,128)(2,1)S(1)}, u32[]{:S(2)}, u32[]{:S(2)}) collective-permute-start(bf16[16,384,128]{2,1,0:T(8,128)(2,1)} %collective-permute-done.2), channel_id=1, source_target_pairs={{0,1},{1,0},{2,3},{3,2},{4,5},{5,4},{6,7},{7,6},{8,9},{9,8},{10,11... | collective-permute-start | bytes 4718600 | tf_op jit(solution)/shard_map/ppermute | solution.py:247
  67.2 33.5 %copy-start.17 = (s32[128]{0:T(128)}, s32[128]{0:T(128)S(1)}, u32[]{:S(2)}) copy-start(s32[128]{0:T(128)S(1)} %and_select_fusion.1.col_ref) | copy-start | bytes 1540
  67.2 6.9 %collective-permute-start.5 = (bf16[640,640]{1,0:T(8,128)(2,1)S(1)}, bf16[640,640]{1,0:T(8,128)(2,1)S(1)}, u32[]{:S(2)}, u32[]{:S(2)}) collective-permute-start(bf16[640,640]{1,0:T(8,128)(2,1)S(1)} %collective-permute-done.4.refs_0_.refs_2_), channel_id=1, source_target_pairs={{8,12},{12,8},{16,20},{20,16},{24,28},{28,24},{9,13},{13,9},{17,21... | collective-permute-start | bytes 2457608 | tf_op jit(solution)/shard_map/ppermute | solution.py:234
  67.9 6.9 %collective-permute-start.12 = (bf16[640,640]{1,0:T(8,128)(2,1)}, bf16[640,640]{1,0:T(8,128)(2,1)S(1)}, u32[]{:S(2)}, u32[]{:S(2)}) collective-permute-start(bf16[640,640]{1,0:T(8,128)(2,1)} %collective-permute-done.8.refs_0_.refs_6_), channel_id=1, source_target_pairs={{16,24},{20,28},{17,25},{21,29},{18,26},{22,30},{19,27},{23,31}} | collective-permute-start | bytes 2457608 | tf_op jit(solution)/shard_map/ppermute | solution.py:237
  68.7 24.5 %collective-permute-start.14 = (bf16[640,640]{1,0:T(8,128)(2,1)}, bf16[640,640]{1,0:T(8,128)(2,1)S(1)}, u32[]{:S(2)}, u32[]{:S(2)}) collective-permute-start(bf16[640,640]{1,0:T(8,128)(2,1)} %collective-permute-done.10.refs_2_.refs_8_), channel_id=1, source_target_pairs={{8,0},{12,4},{9,1},{13,5},{10,2},{14,6},{11,3},{15,7}} | collective-permute-start | bytes 2457608 | tf_op jit(solution)/shard_map/ppermute | solution.py:242
  71.6 34.7 %collective-permute-start.7 = (bf16[640,640]{1,0:T(8,128)(2,1)}, bf16[640,640]{1,0:T(8,128)(2,1)S(1)}, u32[]{:S(2)}, u32[]{:S(2)}) collective-permute-start(bf16[640,640]{1,0:T(8,128)(2,1)} %collective-permute-done.6.refs_2_.refs_4_), channel_id=1, source_target_pairs={{0,4},{4,0},{8,12},{12,8},{16,20},{20,16},{1,5},{5,1},{9,13},{13,9... | collective-permute-start | bytes 2457608 | tf_op jit(solution)/shard_map/ppermute | solution.py:234
  74.0 32.3 %copy-start.5 = (bf16[640,640]{1,0:T(8,128)(2,1)}, bf16[640,640]{1,0:T(8,128)(2,1)S(1)}, u32[]{:S(2)}) copy-start(bf16[640,640]{1,0:T(8,128)(2,1)S(1)} %collective-permute-done.5.refs_1_.refs_3_) | copy-start | bytes 2457604
  74.1 36.9 %collective-permute-start.9 = (bf16[640,640]{1,0:T(8,128)(2,1)}, bf16[640,640]{1,0:T(8,128)(2,1)S(1)}, u32[]{:S(2)}, u32[]{:S(2)}) collective-permute-start(bf16[640,640]{1,0:T(8,128)(2,1)} %collective-permute-done.8.refs_0_.refs_6_), channel_id=1, source_target_pairs={{16,20},{20,16},{24,28},{28,24},{17,21},{21,17},{25,29},{29,25},{1... | collective-permute-start | bytes 2457608 | tf_op jit(solution)/shard_map/ppermute | solution.py:234
  74.8 54.7 %copy-start.6 = (bf16[640,640]{1,0:T(8,128)(2,1)}, bf16[640,640]{1,0:T(8,128)(2,1)S(1)}, u32[]{:S(2)}) copy-start(bf16[640,640]{1,0:T(8,128)(2,1)S(1)} %collective-permute-done.12.refs_0_.refs_10_) | copy-start | bytes 2457604
  74.8 37.5 %collective-permute-start.11 = (bf16[640,640]{1,0:T(8,128)(2,1)}, bf16[640,640]{1,0:T(8,128)(2,1)S(1)}, u32[]{:S(2)}, u32[]{:S(2)}) collective-permute-start(bf16[640,640]{1,0:T(8,128)(2,1)} %collective-permute-done.10.refs_2_.refs_8_), channel_id=1, source_target_pairs={{0,4},{4,0},{8,12},{12,8},{1,5},{5,1},{9,13},{13,9},{2,6},{6,2},{1... | collective-permute-start | bytes 2457608 | tf_op jit(solution)/shard_map/ppermute | solution.py:234
  93.2 36.3 %copy-start.7 = (bf16[640,640]{1,0:T(8,128)(2,1)}, bf16[640,640]{1,0:T(8,128)(2,1)S(1)}, u32[]{:S(2)}) copy-start(bf16[640,640]{1,0:T(8,128)(2,1)S(1)} %collective-permute-done.14.refs_2_.refs_12_) | copy-start | bytes 2457604
  93.2 25.2 %collective-permute-start.13 = (bf16[640,640]{1,0:T(8,128)(2,1)S(1)}, bf16[640,640]{1,0:T(8,128)(2,1)S(1)}, u32[]{:S(2)}, u32[]{:S(2)}) collective-permute-start(bf16[640,640]{1,0:T(8,128)(2,1)S(1)} %collective-permute-done.12.refs_0_.refs_10_), channel_id=1, source_target_pairs={{24,28},{28,24},{25,29},{29,25},{26,30},{30,26},{27,31},{31,27}} | collective-permute-start | bytes 2457608 | tf_op jit(solution)/shard_map/ppermute | solution.py:234
  93.9 35.6 %collective-permute-start.15 = (bf16[640,640]{1,0:T(8,128)(2,1)S(1)}, bf16[640,640]{1,0:T(8,128)(2,1)S(1)}, u32[]{:S(2)}, u32[]{:S(2)}) collective-permute-start(bf16[640,640]{1,0:T(8,128)(2,1)S(1)} %collective-permute-done.14.refs_2_.refs_12_), channel_id=1, source_target_pairs={{0,4},{4,0},{1,5},{5,1},{2,6},{6,2},{3,7},{7,3}} | collective-permute-start | bytes 2457608 | tf_op jit(solution)/shard_map/ppermute | solution.py:234
  106.3 4.6 %copy-start.8 = (bf16[640,640]{1,0:T(8,128)(2,1)}, bf16[640,640]{1,0:T(8,128)(2,1)S(1)}, u32[]{:S(2)}) copy-start(bf16[640,640]{1,0:T(8,128)(2,1)S(1)} %collective-permute-done.7.refs_3_.refs_5_) | copy-start | bytes 2457604
  111.0 7.3 %copy-start.9 = (bf16[640,640]{1,0:T(8,128)(2,1)}, bf16[640,640]{1,0:T(8,128)(2,1)S(1)}, u32[]{:S(2)}) copy-start(bf16[640,640]{1,0:T(8,128)(2,1)S(1)} %collective-permute-done.9.refs_1_.refs_7_) | copy-start | bytes 2457604
  112.3 5.9 %copy-start.10 = (bf16[640,640]{1,0:T(8,128)(2,1)}, bf16[640,640]{1,0:T(8,128)(2,1)S(1)}, u32[]{:S(2)}) copy-start(bf16[640,640]{1,0:T(8,128)(2,1)S(1)} %collective-permute-done.11.refs_3_.refs_9_) | copy-start | bytes 2457604
  118.3 24.1 %copy-start.18 = (s32[2]{0:T(128)S(1)}, s32[2]{0:T(128)}, u32[]{:S(2)}) copy-start(s32[2]{0:T(128)} %param.18) | copy-start | bytes 28
  118.3 14.4 %copy-start.11 = (bf16[640,640]{1,0:T(8,128)(2,1)}, bf16[640,640]{1,0:T(8,128)(2,1)S(1)}, u32[]{:S(2)}) copy-start(bf16[640,640]{1,0:T(8,128)(2,1)S(1)} %collective-permute-done.13.refs_1_.refs_11_) | copy-start | bytes 2457604
  129.4 3.3 %copy-start.12 = (bf16[640,640]{1,0:T(8,128)(2,1)}, bf16[640,640]{1,0:T(8,128)(2,1)S(1)}, u32[]{:S(2)}) copy-start(bf16[640,640]{1,0:T(8,128)(2,1)S(1)} %collective-permute-done.15.refs_3_.refs_13_) | copy-start | bytes 2457604
  133.4 16.0 %all-to-all-start.1 = ((f32[8,3,640]{2,1,0:T(4,128)}), f32[8,3,640]{2,1,0:T(4,128)S(1)}, u32[]{:S(2)}, u32[]{:S(2)}) async-start(f32[8,3,640]{2,1,0:T(4,128)} %add.215), calls=%async_computation.1 | async-start | bytes 163840 | tf_op jit(solution)/shard_map/all_to_all | solution.py:333
  150.1 10.3 %all-to-all-start.2 = ((f32[8,3,640]{2,1,0:T(4,128)}), f32[8,3,640]{2,1,0:T(4,128)S(1)}, u32[]{:S(2)}, u32[]{:S(2)}) async-start(f32[8,3,640]{2,1,0:T(4,128)} %broadcast_in_dim.93), calls=%async_computation.2 | async-start | bytes 163840 | tf_op jit(solution)/shard_map/all_to_all | solution.py:345
  160.5 0.6 copy-start.15
  175.0 2.2 collective-permute-start.16
  175.0 3.3 %collective-permute-start.17 = (bf16[16,128,128]{2,1,0:T(8,128)(2,1)}, bf16[16,128,128]{2,1,0:T(8,128)(2,1)S(1)}, u32[]{:S(2)}, u32[]{:S(2)}) collective-permute-start(bf16[16,128,128]{2,1,0:T(8,128)(2,1)} %get-tuple-element.50), channel_id=1, source_target_pairs={{0,1},{1,0},{2,3},{3,2},{4,5},{5,4},{6,7},{7,6},{8,9},{9,8},{10,11... | collective-permute-start | bytes 1572872 | tf_op jit(solution)/shard_map/ppermute | solution.py:247
  175.5 4.8 %collective-permute-start.18 = (bf16[16,128,128]{2,1,0:T(8,128)(2,1)}, bf16[16,128,128]{2,1,0:T(8,128)(2,1)S(1)}, u32[]{:S(2)}, u32[]{:S(2)}) collective-permute-start(bf16[16,128,128]{2,1,0:T(8,128)(2,1)} %get-tuple-element.52), channel_id=1, source_target_pairs={{0,1},{1,0},{2,3},{3,2},{4,5},{5,4},{6,7},{7,6},{8,9},{9,8},{10,11... | collective-permute-start | bytes 1572872 | tf_op jit(solution)/shard_map/ppermute | solution.py:247
  198.7 8.4 %collective-permute-start.33 = (bf16[16,128,128]{2,1,0:T(8,128)(2,1)}, bf16[16,128,128]{2,1,0:T(8,128)(2,1)S(1)}, u32[]{:S(2)}, u32[]{:S(2)}) collective-permute-start(bf16[16,128,128]{2,1,0:T(8,128)(2,1)} %get-tuple-element.67), channel_id=1, source_target_pairs={{0,1},{1,0},{2,3},{3,2},{4,5},{5,4},{6,7},{7,6},{8,9},{9,8},{10,11... | collective-permute-start | bytes 1572872 | tf_op jit(solution)/shard_map/ppermute | solution.py:247
  198.9 20.3 %collective-permute-start.34 = (bf16[16,128,128]{2,1,0:T(8,128)(2,1)S(1)}, bf16[16,128,128]{2,1,0:T(8,128)(2,1)S(1)}, u32[]{:S(2)}, u32[]{:S(2)}) collective-permute-start(bf16[16,128,128]{2,1,0:T(8,128)(2,1)S(1)} %add_convert_fusion.3), channel_id=1, source_target_pairs={{0,2},{1,3},{2,0},{3,1},{4,6},{5,7},{6,4},{7,5},{8,10},{9,11},{10,... | collective-permute-start | bytes 1572872 | tf_op jit(solution)/shard_map/ppermute | solution.py:247
  206.4 21.0 %collective-permute-start.26 = (bf16[16,128,128]{2,1,0:T(8,128)(2,1)}, bf16[16,128,128]{2,1,0:T(8,128)(2,1)S(1)}, u32[]{:S(2)}, u32[]{:S(2)}) collective-permute-start(bf16[16,128,128]{2,1,0:T(8,128)(2,1)} %get-tuple-element.62), channel_id=1, source_target_pairs={{0,1},{1,0},{2,3},{3,2},{4,5},{5,4},{6,7},{7,6},{8,9},{9,8},{10,11... | collective-permute-start | bytes 1572872 | tf_op jit(solution)/shard_map/ppermute | solution.py:247
  206.6 23.8 %collective-permute-start.27 = (bf16[16,128,128]{2,1,0:T(8,128)(2,1)}, bf16[16,128,128]{2,1,0:T(8,128)(2,1)S(1)}, u32[]{:S(2)}, u32[]{:S(2)}) collective-permute-start(bf16[16,128,128]{2,1,0:T(8,128)(2,1)} %add_convert_fusion.4), channel_id=1, source_target_pairs={{0,2},{1,3},{2,0},{3,1},{4,6},{5,7},{6,4},{7,5},{8,10},{9,11},{10,... | collective-permute-start | bytes 1572872 | tf_op jit(solution)/shard_map/ppermute | solution.py:247
  206.8 29.6 %collective-permute-start.19 = (bf16[16,128,128]{2,1,0:T(8,128)(2,1)}, bf16[16,128,128]{2,1,0:T(8,128)(2,1)S(1)}, u32[]{:S(2)}, u32[]{:S(2)}) collective-permute-start(bf16[16,128,128]{2,1,0:T(8,128)(2,1)} %get-tuple-element.55), channel_id=1, source_target_pairs={{0,1},{1,0},{2,3},{3,2},{4,5},{5,4},{6,7},{7,6},{8,9},{9,8},{10,11... | collective-permute-start | bytes 1572872 | tf_op jit(solution)/shard_map/ppermute | solution.py:247
  207.0 34.3 %collective-permute-start.20 = (bf16[16,128,128]{2,1,0:T(8,128)(2,1)S(1)}, bf16[16,128,128]{2,1,0:T(8,128)(2,1)S(1)}, u32[]{:S(2)}, u32[]{:S(2)}) collective-permute-start(bf16[16,128,128]{2,1,0:T(8,128)(2,1)S(1)} %add_convert_fusion.5), channel_id=1, source_target_pairs={{0,2},{1,3},{2,0},{3,1},{4,6},{5,7},{6,4},{7,5},{8,10},{9,11},{10,... | collective-permute-start | bytes 1572872 | tf_op jit(solution)/shard_map/ppermute | solution.py:247
  219.1 2.2 copy-start.2
  221.3 6.1 %copy-start.14 = (bf16[16,128,128]{2,1,0:T(8,128)(2,1)S(1)}, bf16[16,128,128]{2,1,0:T(8,128)(2,1)}, u32[]{:S(2)}) copy-start(bf16[16,128,128]{2,1,0:T(8,128)(2,1)} %get-tuple-element.61) | copy-start | bytes 1572868
  221.3 9.0 %copy-start.3 = (bf16[16,128,1024]{2,1,0:T(8,128)(2,1)S(1)}, bf16[16,128,1024]{2,1,0:T(8,128)(2,1)}, u32[]{:S(2)}) copy-start(bf16[16,128,1024]{2,1,0:T(8,128)(2,1)} %gather_fusion.2) | copy-start | bytes 12582916
  227.3 20.1 %collective-permute-start.35 = (bf16[2,512,256]{2,1,0:T(8,128)(2,1)S(1)}, bf16[2,512,256]{2,1,0:T(8,128)(2,1)S(1)}, u32[]{:S(2)}, u32[]{:S(2)}) collective-permute-start(bf16[2,512,256]{2,1,0:T(8,128)(2,1)S(1)} %get-tuple-element.70), channel_id=1, source_target_pairs={{0,1},{1,0},{2,3},{3,2},{4,5},{5,4},{6,7},{7,6},{8,9},{9,8},{10,11... | collective-permute-start | bytes 1572872 | tf_op jit(solution)/shard_map/ppermute | solution.py:247
  227.6 8.9 %copy-start.13 = (bf16[16,128,128]{2,1,0:T(8,128)(2,1)S(1)}, bf16[16,128,128]{2,1,0:T(8,128)(2,1)}, u32[]{:S(2)}) copy-start(bf16[16,128,128]{2,1,0:T(8,128)(2,1)} %get-tuple-element.54) | copy-start | bytes 1572868
  236.4 13.0 %collective-permute-start.28 = (bf16[2,512,256]{2,1,0:T(8,128)(2,1)S(1)}, bf16[2,512,256]{2,1,0:T(8,128)(2,1)S(1)}, u32[]{:S(2)}, u32[]{:S(2)}) collective-permute-start(bf16[2,512,256]{2,1,0:T(8,128)(2,1)S(1)} %get-tuple-element.65), channel_id=1, source_target_pairs={{0,1},{1,0},{2,3},{3,2},{4,5},{5,4},{6,7},{7,6},{8,9},{9,8},{10,11... | collective-permute-start | bytes 1572872 | tf_op jit(solution)/shard_map/ppermute | solution.py:247
  247.3 2.6 collective-permute-start.21
  247.6 9.2 %collective-permute-start.36 = (bf16[1,512,256]{2,1,0:T(8,128)(2,1)S(1)}, bf16[1,512,256]{2,1,0:T(8,128)(2,1)S(1)}, u32[]{:S(2)}, u32[]{:S(2)}) collective-permute-start(bf16[1,512,256]{2,1,0:T(8,128)(2,1)S(1)} %fusion.5), channel_id=1, source_target_pairs={{0,2},{1,3},{2,0},{3,1},{4,6},{5,7},{6,4},{7,5},{8,10},{9,11},{10,... | collective-permute-start | bytes 786440 | tf_op jit(solution)/shard_map/ppermute | solution.py:247
  249.5 12.9 %collective-permute-start.29 = (bf16[1,512,256]{2,1,0:T(8,128)(2,1)S(1)}, bf16[1,512,256]{2,1,0:T(8,128)(2,1)S(1)}, u32[]{:S(2)}, u32[]{:S(2)}) collective-permute-start(bf16[1,512,256]{2,1,0:T(8,128)(2,1)S(1)} %fusion.4), channel_id=1, source_target_pairs={{0,2},{1,3},{2,0},{3,1},{4,6},{5,7},{6,4},{7,5},{8,10},{9,11},{10,... | collective-permute-start | bytes 786440 | tf_op jit(solution)/shard_map/ppermute | solution.py:247
  250.0 17.5 %collective-permute-start.22 = (bf16[1,512,256]{2,1,0:T(8,128)(2,1)S(1)}, bf16[1,512,256]{2,1,0:T(8,128)(2,1)S(1)}, u32[]{:S(2)}, u32[]{:S(2)}) collective-permute-start(bf16[1,512,256]{2,1,0:T(8,128)(2,1)S(1)} %fusion.3), channel_id=1, source_target_pairs={{0,2},{1,3},{2,0},{3,1},{4,6},{5,7},{6,4},{7,5},{8,10},{9,11},{10,... | collective-permute-start | bytes 786440 | tf_op jit(solution)/shard_map/ppermute | solution.py:247
  256.8 26.5 %copy-start.1 = (bf16[2,640,1280]{2,1,0:T(8,128)(2,1)S(1)}, bf16[2,640,1280]{2,1,0:T(8,128)(2,1)}, u32[]{:S(2)}) copy-start(bf16[2,640,1280]{2,1,0:T(8,128)(2,1)} %param.17) | copy-start | bytes 9830404
  256.9 10.8 %collective-permute-start.37 = (bf16[4,64,256]{2,1,0:T(8,128)(2,1)S(1)}, bf16[4,64,256]{2,1,0:T(8,128)(2,1)S(1)}, u32[]{:S(2)}, u32[]{:S(2)}) collective-permute-start(bf16[4,64,256]{2,1,0:T(8,128)(2,1)S(1)} %fusion.12), channel_id=1, source_target_pairs={{0,4},{4,0},{8,12},{12,8},{16,20},{20,16},{24,28},{28,24},{1,5},{5... | collective-permute-start | bytes 393224 | tf_op jit(solution)/shard_map/ppermute | solution.py:401
  262.5 5.4 %collective-permute-start.30 = (bf16[4,64,256]{2,1,0:T(8,128)(2,1)S(1)}, bf16[4,64,256]{2,1,0:T(8,128)(2,1)S(1)}, u32[]{:S(2)}, u32[]{:S(2)}) collective-permute-start(bf16[4,64,256]{2,1,0:T(8,128)(2,1)S(1)} %fusion.11), channel_id=1, source_target_pairs={{0,4},{4,0},{8,12},{12,8},{16,20},{20,16},{24,28},{28,24},{1,5},{5... | collective-permute-start | bytes 393224 | tf_op jit(solution)/shard_map/ppermute | solution.py:401
  267.6 5.1 %collective-permute-start.23 = (bf16[4,64,256]{2,1,0:T(8,128)(2,1)S(1)}, bf16[4,64,256]{2,1,0:T(8,128)(2,1)S(1)}, u32[]{:S(2)}, u32[]{:S(2)}) collective-permute-start(bf16[4,64,256]{2,1,0:T(8,128)(2,1)S(1)} %fusion.10), channel_id=1, source_target_pairs={{0,4},{4,0},{8,12},{12,8},{16,20},{20,16},{24,28},{28,24},{1,5},{5... | collective-permute-start | bytes 393224 | tf_op jit(solution)/shard_map/ppermute | solution.py:401
  267.8 5.1 %collective-permute-start.38 = (bf16[2,64,256]{2,1,0:T(8,128)(2,1)S(1)}, bf16[2,64,256]{2,1,0:T(8,128)(2,1)S(1)}, u32[]{:S(2)}, u32[]{:S(2)}) collective-permute-start(bf16[2,64,256]{2,1,0:T(8,128)(2,1)S(1)} %fusion.21), channel_id=1, source_target_pairs={{0,8},{4,12},{8,0},{12,4},{16,24},{20,28},{24,16},{28,20},{1,9},{5... | collective-permute-start | bytes 196616 | tf_op jit(solution)/shard_map/ppermute | solution.py:401
  267.9 6.3 %collective-permute-start.31 = (bf16[2,64,256]{2,1,0:T(8,128)(2,1)S(1)}, bf16[2,64,256]{2,1,0:T(8,128)(2,1)S(1)}, u32[]{:S(2)}, u32[]{:S(2)}) collective-permute-start(bf16[2,64,256]{2,1,0:T(8,128)(2,1)S(1)} %fusion.20), channel_id=1, source_target_pairs={{0,8},{4,12},{8,0},{12,4},{16,24},{20,28},{24,16},{28,20},{1,9},{5... | collective-permute-start | bytes 196616 | tf_op jit(solution)/shard_map/ppermute | solution.py:401
  272.8 4.6 %collective-permute-start.24 = (bf16[2,64,256]{2,1,0:T(8,128)(2,1)S(1)}, bf16[2,64,256]{2,1,0:T(8,128)(2,1)S(1)}, u32[]{:S(2)}, u32[]{:S(2)}) collective-permute-start(bf16[2,64,256]{2,1,0:T(8,128)(2,1)S(1)} %fusion.19), channel_id=1, source_target_pairs={{0,8},{4,12},{8,0},{12,4},{16,24},{20,28},{24,16},{28,20},{1,9},{5... | collective-permute-start | bytes 196616 | tf_op jit(solution)/shard_map/ppermute | solution.py:401
  272.9 5.1 %collective-permute-start.39 = (bf16[1,64,256]{2,1,0:T(8,128)(2,1)S(1)}, bf16[1,64,256]{2,1,0:T(8,128)(2,1)S(1)}, u32[]{:S(2)}, u32[]{:S(2)}) collective-permute-start(bf16[1,64,256]{2,1,0:T(8,128)(2,1)S(1)} %fusion.27), channel_id=1, source_target_pairs={{0,16},{4,20},{8,24},{12,28},{16,0},{20,4},{24,8},{28,12},{1,17},{... | collective-permute-start | bytes 98312 | tf_op jit(solution)/shard_map/ppermute | solution.py:401
  274.2 5.9 %collective-permute-start.32 = (bf16[1,64,256]{2,1,0:T(8,128)(2,1)S(1)}, bf16[1,64,256]{2,1,0:T(8,128)(2,1)S(1)}, u32[]{:S(2)}, u32[]{:S(2)}) collective-permute-start(bf16[1,64,256]{2,1,0:T(8,128)(2,1)S(1)} %fusion.26), channel_id=1, source_target_pairs={{0,16},{4,20},{8,24},{12,28},{16,0},{20,4},{24,8},{28,12},{1,17},{... | collective-permute-start | bytes 98312 | tf_op jit(solution)/shard_map/ppermute | solution.py:401
  277.4 5.2 %collective-permute-start.25 = (bf16[1,64,256]{2,1,0:T(8,128)(2,1)S(1)}, bf16[1,64,256]{2,1,0:T(8,128)(2,1)S(1)}, u32[]{:S(2)}, u32[]{:S(2)}) collective-permute-start(bf16[1,64,256]{2,1,0:T(8,128)(2,1)S(1)} %fusion.25), channel_id=1, source_target_pairs={{0,16},{4,20},{8,24},{12,28},{16,0},{20,4},{24,8},{28,12},{1,17},{... | collective-permute-start | bytes 98312 | tf_op jit(solution)/shard_map/ppermute | solution.py:401
